TPU v7x, 768 devices: a whole 4x8x12 slice. The times are simulated.
768 devices in a mesh: seq: 64 (over y, x, core), head: 12 (over z).
Axes of the slice: x: 4, y: 8, z: 12, core: 2. Of those that a mesh axis runs over, the one named last changes fastest.
Arguments:
- lin_query: bfloat16 [8192, 6144], P('seq', 'head'), may hold values from -0.52734375 to 0.52734375
- lin_key: bfloat16 [8192, 6144], P('seq', 'head'), may hold values from -0.52734375 to 0.52734375
- lin_value: bfloat16 [8192, 6144], P('seq', 'head'), may hold values from -6 to 6
- log_decay: float32 [48, 8192], P('head', 'seq'), may hold values from -1.5 to 0
- out_gate: bfloat16 [8192, 6144], P('seq', 'head'), may hold values from -8 to 8
- norm_gain: float32 [6144], P('head'), may hold values from 0.25 to 1.75
- soft_query: bfloat16 [8192, 6144], P('seq', 'head'), may hold values from -8 to 8
- soft_key: bfloat16 [8192, 768], P('seq'), may hold values from -6 to 6
- soft_value: bfloat16 [8192, 768], P('seq'), may hold values from -6 to 6
- segment_of: int32 [64], replicated, may hold values from 0 to 63, each once
Outputs:
- lin_out: bfloat16 [8192, 6144], P('seq', 'head')
- soft_out: bfloat16 [8192, 6144], P('seq', 'head')
Inputs may be any that keep to these rules, and one draw needn't show every extreme that they name: `segment_of`: each segment number stands once.
All inputs are finite; a program needn't handle non-finite values.
Results may differ from a plain program's by a relative error of at most 0.008.
Values may be sent and summed in bfloat16 or wider, within the bound.
No kernel may reach another device: no remote copies, remote signals or barrier semaphores. Data moves between devices by JAX's collectives and lax.ppermute only.
A program may use at most 128 MiB of HBM per device.

v0:
```python
import jax
import jax.numpy as jnp
from jax import lax
from jax.sharding import PartitionSpec as P

HEAD_DIM = 128
HEADS_DEV = 4
Q_PER_KV = 8


norm_eps = 1e-06


def entering(array, axis, join, neutral):
    place = lax.axis_index(axis)
    gathered = jax.tree.map(
        lambda a, kind: lax.all_gather(a.astype(kind), axis), array, (jnp.bfloat16, jnp.bfloat16)
    )
    state = jax.tree.map(lambda a, e: jnp.zeros_like(a) + jnp.asarray(e, a.dtype), array, neutral)

    def one(hop, state):
        return join(
            state,
            jax.tree.map(
                lambda a, own: lax.dynamic_index_in_dim(a, hop, 0, False).astype(own.dtype),
                gathered,
                array,
            ),
        )

    return lax.fori_loop(0, place, one, state)


def decay_weights(cumulative):
    row_count = cumulative.shape[1]
    positions = jnp.arange(row_count, dtype=jnp.int32)
    causal_mask = positions[:, None] >= positions[None, :]
    spread = cumulative[:, :, None] - cumulative[:, None, :]
    return jnp.where(causal_mask[None], jnp.exp(jnp.where(causal_mask[None], spread, 0.0)), 0.0)


def combine_memory(earlier_part, later_part):
    return (
        jnp.exp(later_part[1])[:, None, None] * earlier_part[0] + later_part[0],
        earlier_part[1] + later_part[1],
    )


def shards(
    lin_query,
    lin_key,
    lin_value,
    log_decay,
    out_gate,
    norm_gain,
    soft_query,
    soft_key,
    soft_value,
    segment_of,
):
    tokens = lin_query.shape[0]
    query_heads = lin_query.reshape(tokens, HEADS_DEV, HEAD_DIM)
    key_heads = lin_key.reshape(tokens, HEADS_DEV, HEAD_DIM)
    value_heads = lin_value.reshape(tokens, HEADS_DEV, HEAD_DIM)
    cumulative = jnp.cumsum(log_decay, axis=1)
    scores = jnp.einsum("thd,shd->hts", query_heads, key_heads, preferred_element_type=jnp.float32)
    mixing = (scores * decay_weights(cumulative)).astype(jnp.bfloat16)
    inside = jnp.einsum("hts,shd->thd", mixing, value_heads, preferred_element_type=jnp.float32)
    tail_decay = jnp.exp(cumulative[:, -1:] - cumulative)
    weighted_keys = key_heads.astype(jnp.float32) * tail_decay.T[:, :, None]
    local_memory = jnp.einsum(
        "thd,the->hde",
        weighted_keys,
        value_heads.astype(jnp.float32),
        precision=lax.Precision.HIGHEST,
    )
    block_log = cumulative[:, -1]
    memory_prev, log_prev = entering(
        (local_memory, block_log),
        "seq",
        combine_memory,
        (jnp.zeros_like(local_memory), jnp.zeros_like(block_log)),
    )
    lifted = query_heads.astype(jnp.float32) * jnp.exp(cumulative).T[:, :, None]
    earlier_term = jnp.einsum("thd,hde->the", lifted, memory_prev, precision=lax.Precision.HIGHEST)
    mixed_out = inside + earlier_term
    square_sums = jnp.sum(mixed_out * mixed_out, axis=(1, 2))
    all_squares = lax.psum(square_sums, "head")
    width_all = HEADS_DEV * HEAD_DIM * lax.axis_size("head")
    inverse_rms = lax.rsqrt(all_squares / width_all + norm_eps)
    flattened = mixed_out.reshape(tokens, HEADS_DEV * HEAD_DIM)
    lin_out = (
        flattened
        * inverse_rms[:, None]
        * norm_gain[None, :]
        * jax.nn.sigmoid(out_gate.astype(jnp.float32))
    ).astype(jnp.bfloat16)
    own_index = lax.axis_index("seq")
    segment_range = jnp.arange(segment_of.shape[0], dtype=jnp.int32)
    own_segment = jnp.sum(jnp.where(segment_range == own_index, segment_of, 0))
    local_rows = jnp.arange(tokens, dtype=jnp.int32)
    query_pos = own_segment * tokens + local_rows
    soft_heads = soft_query.reshape(tokens, HEADS_DEV, HEAD_DIM)
    score_scale = HEAD_DIM ** (-0.5)
    shared_index = lax.axis_index("head") * HEADS_DEV // Q_PER_KV
    own_keys = lax.dynamic_slice_in_dim(soft_key, shared_index * HEAD_DIM, HEAD_DIM, 1)
    own_values = lax.dynamic_slice_in_dim(soft_value, shared_index * HEAD_DIM, HEAD_DIM, 1)
    key_piece = lax.all_gather(own_keys, "seq", axis=0, tiled=True)
    value_piece = lax.all_gather(own_values, "seq", axis=0, tiled=True)
    row_count = key_piece.shape[0]
    row_ids = jnp.arange(row_count, dtype=jnp.int32)
    owners = row_ids // tokens
    key_segments = jnp.sum(
        jnp.where(owners[:, None] == segment_range[None, :], segment_of[None, :], 0), axis=1
    )
    key_pos = key_segments * tokens + row_ids % tokens
    visible = (key_pos[None, :] <= query_pos[:, None])[None]
    raw_logits = jnp.einsum(
        "tgd,sd->gts", soft_heads, key_piece, preferred_element_type=jnp.float32
    )
    old_max = jnp.full((HEADS_DEV, tokens), -1e30, jnp.float32)
    piece_max = jnp.max(jnp.where(visible, raw_logits * score_scale, -1e30), axis=2)
    new_max = jnp.maximum(old_max, piece_max)
    weights_now = jnp.where(visible, jnp.exp(raw_logits * score_scale - new_max[:, :, None]), 0.0)
    piece_total = jnp.sum(weights_now, axis=2)
    weights_low = weights_now.astype(jnp.bfloat16)
    new_acc = jnp.einsum(
        "gts,sd->gtd", weights_low, value_piece, preferred_element_type=jnp.float32
    )
    normalized = new_acc / piece_total[:, :, None]
    soft_out = (
        normalized.transpose(1, 0, 2).reshape(tokens, HEADS_DEV * HEAD_DIM).astype(jnp.bfloat16)
    )
    return (lin_out, soft_out)


def solution(mesh):
    return jax.shard_map(
        shards,
        mesh=mesh,
        in_specs=(
            P("seq", "head"),
            P("seq", "head"),
            P("seq", "head"),
            P("head", "seq"),
            P("seq", "head"),
            P("head"),
            P("seq", "head"),
            P("seq", None),
            P("seq", None),
            P(),
        ),
        out_specs=(P("seq", "head"), P("seq", "head")),
        check_vma=False,
    )
```

profile of v0, /device:TPU:62, one launch (start us, length us, event | category | flops | bytes accessed | tf_op | source)
XLA Modules:
  0.0 385.8 jit_solution(9727916759206456701)
XLA Ops:
  10.3 1.0 copy.59
  12.6 1.8 convolution_convert_fusion
  14.5 1.3 fusion.63
  16.4 1.3 dynamic-slice
  18.8 126.8 %all-reduce = bf16[256]{0:T(256)(128)(2,1)S(1)} all-reduce(bf16[256]{0:T(256)(128)(2,1)S(1)} %dynamic-update-slice), channel_id=2, replica_groups=mesh['seq'=64,'head'=12] {'seq'}, use_global_device_ids=true, to_apply=%add | all-reduce | flops 256 | bytes 1024
  145.7 1.1 select_reduce_fusion
  146.8 1.3 convolution_bitcast_fusion.1
  148.1 3.7 broadcast_compare_fusion
  151.9 3.8 fusion
  155.7 5.7 %copy-done.1 = f32[8192,128,4]{1,0,2:T(8,128)} copy-done((f32[8192,128,4]{1,0,2:T(8,128)}, f32[8192,128,4]{1,0,2:T(8,128)S(1)}, u32[]{:S(2)}) %copy-start.1) | copy-done | bytes 16777240
  161.4 3.6 fusion.3
  165.0 26.1 %all-gather.8.cloned.1.call-done = bf16[8192,128]{0,1:T(8,128)(2,1)} async-done(((bf16[128,128]{0,1:T(8,128)(2,1)}), bf16[8192,128]{0,1:T(8,128)(2,1)}) %all-gather.8.cloned.1.call-update) | async-done | bytes 2097168 | tf_op jit(solution)/shard_map/all_gather | solution.py:109
  191.1 9.6 %fusion.23 = bf16[128,4,128]{0,2,1:T(8,128)(2,1)S(1)} fusion(f32[8192,128,4]{1,0,2:T(8,128)} %copy-done.1, f32[4,128]{1,0:T(4,128)S(1)} %broadcast_maximum_fusion, pred[128,8192]{0,1:T(8,128)(4,1)S(1)} %broadcast_compare_fusion, bf16[8192,128]{0,1:T(8,128)(2,1)} %all-gather.8.cloned.1.call-done, f32[128,4]{0,1:T(4,128)S(1)} %bitcast.111), kind=kOutput, calls=%fused_computation.25 | convolution fusion | flops 1090650112 | bytes 20058112 | tf_op jit(solution)/shard_map/gts,sd->gtd/dot_general | solution.py:127
  201.4 84.8 %all-gather.10.cloned.1.call-done = bf16[256,128,128]{2,1,0:T(8,128)(2,1)} async-done(((bf16[4,128,128]{2,1,0:T(8,128)(2,1)}), bf16[256,128,128]{2,1,0:T(8,128)(2,1)}) %all-gather.10.cloned.1.call-update) | async-done | bytes 8388624 | tf_op jit(solution)/shard_map/all_gather | solution.py:17
  286.2 66.1 %while.12 = (s32[]{:T(128)}, f32[4,128,128]{2,1,0:T(8,128)S(1)}, s32[]{:T(128)}, bf16[64,4]{1,0:T(8,128)(2,1)S(1)}, bf16[64,4,128,128]{3,2,1,0:T(8,128)(2,1)}, /*index=5*/s32[]{:T(128)}, s32[]{:T(128)}, s32[]{:T(128)}) while((s32[]{:T(128)}, f32[4,128,128]{2,1,0:T(8,128)S(1)}, s32[]{:T(128)}, bf16[64,4]{1,0:T(8,128)(2,1)S(1)}, ...), condition=%wide.region_2.3_spmd, body=%wide.region_1.2_spmd.sunk | while | flops 196617 | bytes 655527 | solution.py:31
  286.3 1.0 convert_add_fusion.2
  287.3 1.0 convert_add_fusion.2
  288.4 1.0 convert_add_fusion.2
  289.5 1.0 convert_add_fusion.2
  290.5 1.0 convert_add_fusion.2
  291.6 1.0 convert_add_fusion.2
  292.7 1.0 convert_add_fusion.2
  293.7 1.0 convert_add_fusion.2
  294.8 1.0 convert_add_fusion.2
  295.8 1.0 convert_add_fusion.2
  296.9 1.0 convert_add_fusion.2
  298.0 1.0 convert_add_fusion.2
  299.0 1.0 convert_add_fusion.2
  300.1 1.0 convert_add_fusion.2
  301.2 1.0 convert_add_fusion.2
  302.2 1.0 convert_add_fusion.2
  303.3 1.0 convert_add_fusion.2
  304.4 1.0 convert_add_fusion.2
  305.4 1.0 convert_add_fusion.2
  308.6 1.0 convert_add_fusion.2
  309.7 1.0 convert_add_fusion.2
  310.8 1.0 convert_add_fusion.2
  314.0 1.0 convert_add_fusion.2
  315.0 1.0 convert_add_fusion.2
  316.1 1.0 convert_add_fusion.2
  318.2 1.0 convert_add_fusion.2
  319.3 1.0 convert_add_fusion.2
  320.4 1.0 convert_add_fusion.2
  321.4 1.0 convert_add_fusion.2
  323.6 1.0 convert_add_fusion.2
  324.6 1.0 convert_add_fusion.2
  325.7 1.0 convert_add_fusion.2
  328.9 1.0 convert_add_fusion.2
  330.0 1.0 convert_add_fusion.2
  331.0 1.0 convert_add_fusion.2
  334.2 1.0 convert_add_fusion.2
  335.3 1.0 convert_add_fusion.2
  336.4 1.0 convert_add_fusion.2
  338.5 1.0 convert_add_fusion.2
  339.6 1.0 convert_add_fusion.2
  340.6 1.0 convert_add_fusion.2
  341.7 1.0 convert_add_fusion.2
  343.8 1.0 convert_add_fusion.2
  344.9 1.0 convert_add_fusion.2
  346.0 1.0 convert_add_fusion.2
  349.2 1.0 convert_add_fusion.2
  350.2 1.0 convert_add_fusion.2
  351.3 1.0 convert_add_fusion.2
  353.2 25.3 %psum.7 = f32[128]{0:T(128)S(1)} all-reduce(f32[128]{0:T(128)S(1)} %get-tuple-element.67), channel_id=1, replica_groups=mesh['seq'=64,'head'=12] {'head'}, use_global_device_ids=true, to_apply=%region_4.5 | all-reduce | flops 128 | bytes 1024 | tf_op jit(solution)/shard_map/psum | solution.py:88
  (113 shorter events, 22.5 us)
Async XLA Ops:
  7.2 0.9 copy-start
  7.2 144.7 %all-gather.6.cloned.1.call-start = ((), (), s32[]{:S(2)}) async-start(), calls=%async_computation | async-start | bytes 2129920 | tf_op jit(solution)/shard_map/all_gather | solution.py:108
  8.7 182.3 %all-gather.8.cloned.1.call-start = ((), (), s32[]{:S(2)}) async-start(), calls=%async_computation.1 | async-start | bytes 2129920 | tf_op jit(solution)/shard_map/all_gather | solution.py:109
  10.3 275.9 %all-gather.10.cloned.1.call-start = ((), (), s32[]{:S(2)}) async-start(), calls=%async_computation.2 | async-start | bytes 8519680 | tf_op jit(solution)/shard_map/all_gather | solution.py:17
  155.7 5.7 %copy-start.1 = (f32[8192,128,4]{1,0,2:T(8,128)}, f32[8192,128,4]{1,0,2:T(8,128)S(1)}, u32[]{:S(2)}) copy-start(f32[8192,128,4]{1,0,2:T(8,128)S(1)} %get-tuple-element.70) | copy-start | bytes 50331652
  165.0 187.3 %copy-start.2 = (bf16[128,512]{1,0:T(8,128)(2,1)S(1)}, bf16[128,512]{1,0:T(8,128)(2,1)}, u32[]{:S(2)}) copy-start(bf16[128,512]{1,0:T(8,128)(2,1)} %param.12) | copy-start | bytes 393220
  191.1 187.5 %copy-start.3 = (bf16[128,512]{1,0:T(8,128)(2,1)S(1)}, bf16[128,512]{1,0:T(8,128)(2,1)}, u32[]{:S(2)}) copy-start(bf16[128,512]{1,0:T(8,128)(2,1)} %param.16) | copy-start | bytes 393220
  191.1 187.5 %copy-start.4 = (f32[512]{0:T(512)S(1)}, f32[512]{0:T(512)}, u32[]{:S(2)}) copy-start(f32[512]{0:T(512)} %param.17) | copy-start | bytes 6148
Sparse Core Ops, SparseCore 0:
  12.5 91.5 all-gather.5
  107.9 83.0 all-gather.7
  195.6 90.5 all-gather.9
where the time goes:
time: 387 us; the launch traced here: 386 us
  blocking collectives  152 us (39%)
  waiting for transfers between devices  111 us (29%)
  other arithmetic  75.6 us (20%)
  matrix products  17.3 us (4%)
  between operations  15.2 us (4%)
  local copies, waits for them, and re-layouts  12.6 us (3%)
    unnamed x1, blocking collectives  127 us
    all_gather x1, waiting for transfers between devices, entering(): lax.all_gather(a.astype(kind), axis)  84.8 us
    add x62, other arithmetic, combine_memory(): jnp.exp(later_part[1])[:, None, None] * earlier_part[0] + later_part[0]  63.2 us
    all_gather x1, waiting for transfers between devices, shards(): value_piece = lax.all_gather(own_values, 'seq', axis=0, tiled=True)  26.1 us
    psum x1, blocking collectives, shards(): all_squares = lax.psum(square_sums, 'head')  25.3 us
    dot_general x1, matrix products, shards(): jnp.einsum('gts,sd->gtd', weights_low, value_piece, preferred_element_typ...  9.57 us
    unnamed x15, local copies, waits for them, and re-layouts  9.56 us
  transfers between devices with their start and end apart: 3, of which 2 were waited for; matrix products, arithmetic and copies ran while one was open for 8% of the time, Pallas kernels for 0%

commit v1 on v0

v1 whole, which is shorter than its diff:
```python
import jax
import jax.numpy as jnp
from jax import lax
from jax.experimental import pallas as pl
from jax.experimental.pallas import tpu as pltpu
from jax.sharding import PartitionSpec as P


HEAD_DIM = 128
HEADS_DEV = 4
Q_PER_KV = 8
TOK = 128
SEGS = 64
HALF = 32
ROWS = 8
COLUMNS = 4
KEY_BLOCK = 8

norm_eps = 1e-06
SCALE = HEAD_DIM ** (-0.5)
LOG2E = 1.4426950408889634
F32 = jnp.float32
BF16 = jnp.bfloat16
MASKED = -1e30

VM = pl.BlockSpec(memory_space=pltpu.VMEM)
SM = pl.BlockSpec(memory_space=pltpu.SMEM)


def dot(a, b, ca, cb, precision=None):
    return lax.dot_general(
        a, b, (((ca,), (cb,)), ((), ())), precision=precision, preferred_element_type=F32
    )


def iotas(n=TOK):
    return (
        lax.broadcasted_iota(jnp.int32, (n, TOK), 0),
        lax.broadcasted_iota(jnp.int32, (n, TOK), 1),
    )


def cumulative_columns(log_row):
    row, col = iotas()
    wide = jnp.broadcast_to(log_row, (TOK, TOK))
    column = jnp.sum(jnp.where(col <= row, wide, 0.0), axis=1, keepdims=True)
    log_column = jnp.sum(jnp.where(col == row, wide, 0.0), axis=1, keepdims=True)
    as_row = jnp.sum(jnp.where(row <= col, log_column, 0.0), axis=0, keepdims=True)
    return column, as_row


def split_bf16(value):
    high = value.astype(BF16)
    return high, (value - high.astype(F32)).astype(BF16)


def memory_kernel(key_ref, value_ref, log_ref, out_ref):
    for head in range(HEADS_DEV):
        lanes = slice(head * HEAD_DIM, (head + 1) * HEAD_DIM)
        column, _ = cumulative_columns(log_ref[head : head + 1, :])
        last = column[TOK - 1 :, :]
        weighted = key_ref[:, lanes].astype(F32) * jnp.exp(last - column)
        high, low = split_bf16(weighted)
        value = value_ref[:, lanes]
        local = dot(high, value, 0, 0) + dot(low, value, 0, 0)
        pieces = slice(head * 16, (head + 1) * 16)
        total = jnp.broadcast_to(last, (8, HEAD_DIM))
        first, _ = split_bf16(total)
        second, third = split_bf16(total - first.astype(F32))
        sub = lax.broadcasted_iota(jnp.int32, (8, HEAD_DIM), 0)
        parts = jnp.where(
            sub == 0,
            first.astype(F32),
            jnp.where(sub == 1, second.astype(F32), jnp.where(sub == 2, third.astype(F32), 0.0)),
        )
        both = jnp.concatenate(
            [local.reshape(16, 8, HEAD_DIM), jnp.broadcast_to(parts[None], (16, 8, HEAD_DIM))],
            axis=1,
        )
        out_ref[pieces] = both.astype(BF16)


def scan_kernel(in_ref, out_ref, wide_ref):
    wide_ref[...] = in_ref[...].astype(F32)
    block_log = wide_ref[:, 8, :] + wide_ref[:, 9, :] + wide_ref[:, 10, :]
    row, col = iotas(SEGS)
    later = jnp.where(row > col, block_log, 0.0)
    trow = lax.broadcasted_iota(jnp.int32, (SEGS, SEGS), 0)
    tcol = lax.broadcasted_iota(jnp.int32, (SEGS, SEGS), 1)
    before = jnp.where(tcol < trow, 1.0, 0.0)
    spread = dot(before, later, 1, 0, lax.Precision.HIGHEST)[:, :SEGS]
    decay = jnp.where(tcol < trow, jnp.exp(spread), 0.0)
    high, low = split_bf16(decay)
    for sub in range(8):
        data = wide_ref[:, sub, :].astype(BF16)
        wide_ref[:, sub, :] = dot(high, data, 1, 0) + dot(low, data, 1, 0)
    out_ref[...] = wide_ref[:, 0:8, :].astype(BF16)


def inside_kernel(query_ref, key_ref, value_ref, log_ref, out_ref):
    row, col = iotas()
    for head in range(HEADS_DEV):
        lanes = slice(head * HEAD_DIM, (head + 1) * HEAD_DIM)
        column, as_row = cumulative_columns(log_ref[head : head + 1, :])
        scores = dot(query_ref[:, lanes], key_ref[:, lanes], 1, 1)
        causal = col <= row
        decay = jnp.exp(jnp.where(causal, column - as_row, 0.0))
        mixing = jnp.where(causal, scores * decay, 0.0).astype(BF16)
        out_ref[:, lanes] = dot(mixing, value_ref[:, lanes], 1, 0)


def mixed_kernel(query_ref, log_ref, inside_ref, memory_ref, out_ref, square_ref):
    row, col = iotas()
    squares = jnp.zeros((TOK, HEAD_DIM), F32)
    for head in range(HEADS_DEV):
        lanes = slice(head * HEAD_DIM, (head + 1) * HEAD_DIM)
        column, _ = cumulative_columns(log_ref[head : head + 1, :])
        memory = memory_ref[head * 16 : (head + 1) * 16].astype(F32).reshape(HEAD_DIM, HEAD_DIM)
        earlier = dot(query_ref[:, lanes], memory.astype(BF16), 1, 0)
        mixed = inside_ref[:, lanes] + jnp.exp(column) * earlier
        out_ref[:, lanes] = mixed
        squares = squares + mixed * mixed
    total = jnp.sum(squares, axis=1, keepdims=True)
    total_row = jnp.sum(jnp.where(row == col, total, 0.0), axis=0, keepdims=True)
    square_ref[...] = jnp.broadcast_to(total_row[None], square_ref.shape)


def gate_kernel(mixed_ref, square_ref, gain_ref, gate_ref, out_ref):
    row, col = iotas()
    shards = square_ref.shape[0]
    total_row = square_ref[0, 0:1, :]
    for shard in range(1, shards):
        total_row = total_row + square_ref[shard, 0:1, :]
    total = jnp.sum(jnp.where(row == col, total_row, 0.0), axis=1, keepdims=True)
    inverse = lax.rsqrt(total / (HEADS_DEV * HEAD_DIM * shards) + norm_eps)
    gated = mixed_ref[...] * inverse * gain_ref[...] * jax.nn.sigmoid(gate_ref[...].astype(F32))
    out_ref[...] = gated.astype(BF16)


def pieces_kernel(place_ref, key_ref, value_ref, out_ref):
    out_ref[:, :, 0:HEAD_DIM] = jnp.broadcast_to(key_ref[...][None], (ROWS, TOK, HEAD_DIM))
    out_ref[:, :, HEAD_DIM:] = jnp.broadcast_to(value_ref[...][None], (ROWS, TOK, HEAD_DIM))


def attend(place, core, seg_ref, own_segment, query_ref, pairs_ref, state):
    def block(step, state):
        column = jnp.bitwise_and(place // 2 - step, COLUMNS - 1)
        rows = pairs_ref[pl.ds(step * KEY_BLOCK, KEY_BLOCK)]
        keys = rows[:, :, 0:HEAD_DIM].reshape(KEY_BLOCK * TOK, HEAD_DIM)
        values = rows[:, :, HEAD_DIM:].reshape(KEY_BLOCK * TOK, HEAD_DIM)
        shift = []
        for at in range(KEY_BLOCK):
            seg = seg_ref[at * ROWS + column * 2 + core]
            shift.append(jnp.where(seg < own_segment, 0.0, MASKED).astype(F32))
        new_state = []
        for head in range(HEADS_DEV):
            peak, total, acc = state[head]
            query = query_ref[:, head * HEAD_DIM : (head + 1) * HEAD_DIM]
            logits = dot(query, keys, 1, 1)
            parts = [logits[:, at * TOK : (at + 1) * TOK] + shift[at] for at in range(KEY_BLOCK)]
            top = parts[0]
            for part in parts[1:]:
                top = jnp.maximum(top, part)
            new_peak = jnp.maximum(peak, jnp.max(top, axis=1, keepdims=True))
            fade = jnp.exp2((peak - new_peak) * (SCALE * LOG2E))
            weights = [jnp.exp2((part - new_peak) * (SCALE * LOG2E)) for part in parts]
            summed = weights[0]
            for part in weights[1:]:
                summed = summed + part
            low = jnp.concatenate([part.astype(BF16) for part in weights], axis=1)
            new_state.append(
                (new_peak, total * fade + summed, acc * fade + dot(low, values, 1, 0))
            )
        return tuple(new_state)

    return lax.fori_loop(0, HALF // KEY_BLOCK, block, state)


def first_kernel(
    seg_ref, place_ref, query_ref, own_ref, pairs_ref, acc_ref, total_ref, peak_ref
):
    place = place_ref[0]
    own_segment = seg_ref[place]
    row, col = iotas()
    keys = own_ref[0, :, 0:HEAD_DIM]
    values = own_ref[0, :, HEAD_DIM:]
    state = []
    for head in range(HEADS_DEV):
        query = query_ref[:, head * HEAD_DIM : (head + 1) * HEAD_DIM]
        logits = jnp.where(col <= row, dot(query, keys, 1, 1), MASKED)
        peak = jnp.max(logits, axis=1, keepdims=True)
        weights = jnp.exp2((logits - peak) * (SCALE * LOG2E))
        state.append((peak, weights, dot(weights.astype(BF16), values, 1, 0)))
    state = attend(place, place % 2, seg_ref, own_segment, query_ref, pairs_ref, tuple(state))
    for head in range(HEADS_DEV):
        peak, total, acc = state[head]
        acc_ref[head] = acc
        total_ref[head] = total
        peak_ref[head] = jnp.broadcast_to(peak, (TOK, HEAD_DIM))


def second_kernel(
    seg_ref, place_ref, query_ref, pairs_ref, acc_ref, total_ref, peak_ref, out_ref
):
    place = place_ref[0]
    own_segment = seg_ref[place]
    state = tuple(
        (peak_ref[head][:, 0:1], total_ref[head], acc_ref[head]) for head in range(HEADS_DEV)
    )
    state = attend(place, 1 - place % 2, seg_ref, own_segment, query_ref, pairs_ref, state)
    for head in range(HEADS_DEV):
        _, total, acc = state[head]
        lanes = slice(head * HEAD_DIM, (head + 1) * HEAD_DIM)
        out_ref[:, lanes] = (acc / jnp.sum(total, axis=1, keepdims=True)).astype(BF16)


def shape(*dims, dtype=F32):
    return jax.ShapeDtypeStruct(dims, dtype)


def local_memory(key, value, log_decay):
    return pl.pallas_call(
        memory_kernel, name="memory", out_shape=shape(SEGS, 16, HEAD_DIM, dtype=BF16),
        in_specs=[VM] * 3, out_specs=VM,
    )(key, value, log_decay)


def scan_memory(received):
    return pl.pallas_call(
        scan_kernel, name="scan", out_shape=shape(SEGS, 8, HEAD_DIM, dtype=BF16),
        in_specs=[VM], out_specs=VM, scratch_shapes=[pltpu.VMEM((SEGS, 16, HEAD_DIM), F32)],
    )(received)


def inside_part(query, key, value, log_decay):
    return pl.pallas_call(
        inside_kernel, name="inside", out_shape=shape(TOK, HEADS_DEV * HEAD_DIM),
        in_specs=[VM] * 4, out_specs=VM,
    )(query, key, value, log_decay)


def mixed_part(query, log_decay, inside, memory, shards):
    return pl.pallas_call(
        mixed_kernel, name="mixed",
        out_shape=(shape(TOK, HEADS_DEV * HEAD_DIM), shape(shards, 8, TOK)),
        in_specs=[VM] * 4, out_specs=(VM, VM),
    )(query, log_decay, inside, memory)


def gate_part(mixed, squares, gain, gate):
    return pl.pallas_call(
        gate_kernel, name="gate", out_shape=shape(TOK, HEADS_DEV * HEAD_DIM, dtype=BF16),
        in_specs=[VM] * 4, out_specs=VM,
    )(mixed, squares, gain[None, :], gate)


def key_value_pieces(place, key, value):
    return pl.pallas_call(
        pieces_kernel, name="pieces",
        out_shape=shape(ROWS, TOK, 2 * HEAD_DIM, dtype=BF16),
        grid_spec=pltpu.PrefetchScalarGridSpec(
            num_scalar_prefetch=1,
            grid=(1,),
            in_specs=[
                pl.BlockSpec((TOK, HEAD_DIM), lambda i, at: (0, at[0])),
                pl.BlockSpec((TOK, HEAD_DIM), lambda i, at: (0, at[0])),
            ],
            out_specs=pl.BlockSpec((ROWS, TOK, 2 * HEAD_DIM), lambda i, at: (0, 0, 0)),
        ),
    )(place, key, value)


def attend_first(segment_of, place, query, pieces, pairs):
    return pl.pallas_call(
        first_kernel, name="attend_first",
        out_shape=(shape(HEADS_DEV, TOK, HEAD_DIM),) * 3,
        grid=(1,),
        in_specs=[
            SM, SM,
            pl.BlockSpec((TOK, HEADS_DEV * HEAD_DIM), lambda i: (0, 0)),
            pl.BlockSpec((1, TOK, 2 * HEAD_DIM), lambda i: (0, 0, 0)),
            pl.BlockSpec((HALF, TOK, 2 * HEAD_DIM), lambda i: (0, 0, 0)),
        ],
        out_specs=(pl.BlockSpec((HEADS_DEV, TOK, HEAD_DIM), lambda i: (0, 0, 0)),) * 3,
    )(segment_of, place, query, pieces, pairs)


def attend_second(segment_of, place, query, pairs, state):
    return pl.pallas_call(
        second_kernel, name="attend_second",
        out_shape=shape(TOK, HEADS_DEV * HEAD_DIM, dtype=BF16),
        in_specs=[SM, SM] + [VM] * 5, out_specs=VM,
    )(segment_of, place, query, pairs, *state)


def shards(
    lin_query,
    lin_key,
    lin_value,
    log_decay,
    out_gate,
    norm_gain,
    soft_query,
    soft_key,
    soft_value,
    segment_of,
):
    place = lax.axis_index("seq").astype(jnp.int32)[None]
    shared = (lax.axis_index("head") * HEADS_DEV // Q_PER_KV).astype(jnp.int32)[None]
    head_shards = lax.axis_size("head")
    same_column = [[row * 8 + at for row in range(ROWS)] for at in range(8)]
    shifts = [
        [(at, at // 8 * 8 + (at + 2 * step) % 8) for at in range(SEGS)] for step in range(COLUMNS)
    ]
    partners = [(at, at ^ 1) for at in range(SEGS)]
    pieces = key_value_pieces(shared, soft_key, soft_value)
    column = lax.all_to_all(
        pieces, "seq", 0, 0, tiled=True, axis_index_groups=same_column
    )
    columns = [column] + [lax.ppermute(column, "seq", shifts[step]) for step in range(1, COLUMNS)]
    pairs = jnp.concatenate(columns, axis=0)
    local = local_memory(lin_key, lin_value, log_decay)
    received = lax.all_to_all(local, "seq", 0, 0, tiled=True)
    scanned = scan_memory(received)
    memory = lax.all_to_all(scanned, "seq", 0, 0, tiled=True)
    inside = inside_part(lin_query, lin_key, lin_value, log_decay)
    mixed, squares = mixed_part(lin_query, log_decay, inside, memory, head_shards)
    squares = lax.all_to_all(squares, "head", 0, 0, tiled=True)
    lin_out = gate_part(mixed, squares, norm_gain, out_gate)
    others = lax.ppermute(pairs, "seq", partners)
    state = attend_first(segment_of, place, soft_query, pieces, pairs)
    soft_out = attend_second(segment_of, place, soft_query, others, state)
    return (lin_out, soft_out)


def solution(mesh):
    return jax.shard_map(
        shards,
        mesh=mesh,
        in_specs=(
            P("seq", "head"),
            P("seq", "head"),
            P("seq", "head"),
            P("head", "seq"),
            P("seq", "head"),
            P("head"),
            P("seq", "head"),
            P("seq", None),
            P("seq", None),
            P(),
        ),
        out_specs=(P("seq", "head"), P("seq", "head")),
        check_vma=False,
    )
```

time: 387 us -> 149 us (0.39)
  the two profiles are of different devices: /device:TPU:62 before, /device:TPU:1 now
where the time goes in v1:
time: 149 us
  blocking collectives  39.2 us (26%)
  starting transfers between devices  37.6 us (25%)
  waiting for transfers between devices  37 us (25%)
  Pallas kernels  32.6 us (22%)
    all_to_all x1, blocking collectives, shards(): lax.all_to_all(pieces, 'seq', 0, 0, tiled=True, axis_index_groups=same_co...  19.9 us
    all_to_all x1, blocking collectives, shards(): received = lax.all_to_all(local, 'seq', 0, 0, tiled=True)  19.4 us
    ppermute x3, waiting for transfers between devices, shards(): lax.ppermute(column, 'seq', shifts[step])  18.7 us
    all_to_all x1, starting transfers between devices, shards(): squares = lax.all_to_all(squares, 'head', 0, 0, tiled=True)  14.9 us
    ppermute x3, starting transfers between devices, shards(): lax.ppermute(column, 'seq', shifts[step])  14.4 us
    pallas_call x1, Pallas kernels, attend_second(): pl.pallas_call(second_kernel, name='attend_second', out_shape=shape(TOK,...  10.2 us
    pallas_call x1, Pallas kernels, attend_first(): pl.pallas_call(first_kernel, name='attend_first', out_shape=(shape(HEADS_...  10.2 us
    all_to_all x1, waiting for transfers between devices, shards(): squares = lax.all_to_all(squares, 'head', 0, 0, tiled=True)  9.68 us
  transfers between devices with their start and end apart: 6, of which 5 were waited for; matrix products, arithmetic and copies ran while one was open for 0% of the time, Pallas kernels for 14%

profile of v1, /device:TPU:1, one launch (start us, length us, event | category | flops | bytes accessed | tf_op | source)
XLA Modules:
  0.0 148.6 jit_solution(8117080231787101481)
XLA Ops:
  0.7 1.6 %pieces.1.own_ref = bf16[8,128,256]{2,1,0:T(8,128)(2,1)} custom-call(s32[1]{0:T(128)} %bitcast.2.place_ref, bf16[128,768]{1,0:T(8,128)(2,1)} %key_ref.5, bf16[128,768]{1,0:T(8,128)(2,1)} %value_ref.5), custom_call_target="tpu_custom_call" | custom-call | tf_op jit(solution)/shard_map/pieces/pallas_call | solution.py:258
  2.3 19.9 %all_to_all.20 = bf16[8,128,256]{2,1,0:T(8,128)(2,1)S(1)} all-to-all(bf16[8,128,256]{2,1,0:T(8,128)(2,1)} %pieces.1.own_ref), channel_id=1, replica_groups={{0,96,192,288,384,480,576,672},{12,108,204,300,396,492,588,684},{24,120..., dimensions={0} | all-to-all | bytes 1048576 | tf_op jit(solution)/shard_map/all_to_all | solution.py:317
  22.2 7.0 %collective-permute-start = (bf16[8,128,256]{2,1,0:T(8,128)(2,1)S(1)}, bf16[8,128,256]{2,1,0:T(8,128)(2,1)S(1)}, u32[]{:S(2)}, u32[]{:S(2)}) collective-permute-start(bf16[8,128,256]{2,1,0:T(8,128)(2,1)S(1)} %all_to_all.20), channel_id=1, source_target_pairs={{0,24},{12,36},{24,48},{36,60},{48,72},{60,84},{72,0},{84,12},{96,... | collective-permute-start | bytes 1572872 | tf_op jit(solution)/shard_map/ppermute | solution.py:320
  29.2 4.4 %collective-permute-start.1 = (bf16[8,128,256]{2,1,0:T(8,128)(2,1)S(1)}, bf16[8,128,256]{2,1,0:T(8,128)(2,1)S(1)}, u32[]{:S(2)}, u32[]{:S(2)}) collective-permute-start(bf16[8,128,256]{2,1,0:T(8,128)(2,1)S(1)} %all_to_all.20), channel_id=1, source_target_pairs={{0,48},{12,60},{24,72},{36,84},{48,0},{60,12},{72,24},{84,36},{96,... | collective-permute-start | bytes 1572872 | tf_op jit(solution)/shard_map/ppermute | solution.py:320
  33.5 3.1 %collective-permute-start.2 = (bf16[8,128,256]{2,1,0:T(8,128)(2,1)S(1)}, bf16[8,128,256]{2,1,0:T(8,128)(2,1)S(1)}, u32[]{:S(2)}, u32[]{:S(2)}) collective-permute-start(bf16[8,128,256]{2,1,0:T(8,128)(2,1)S(1)} %all_to_all.20), channel_id=1, source_target_pairs={{0,72},{12,84},{24,0},{36,12},{48,24},{60,36},{72,48},{84,60},{96,... | collective-permute-start | bytes 1572872 | tf_op jit(solution)/shard_map/ppermute | solution.py:320
  36.6 2.2 %collective-permute-done = bf16[8,128,256]{2,1,0:T(8,128)(2,1)S(1)} collective-permute-done((bf16[8,128,256]{2,1,0:T(8,128)(2,1)S(1)}, bf16[8,128,256]{2,1,0:T(8,128)(2,1)S(1)}, u32[]{:S(2)}, u32[]{:S(2)}) %collective-permute-start) | collective-permute-done | bytes 524320 | tf_op jit(solution)/shard_map/ppermute | solution.py:320
  38.9 13.6 %collective-permute-done.1 = bf16[8,128,256]{2,1,0:T(8,128)(2,1)S(1)} collective-permute-done((bf16[8,128,256]{2,1,0:T(8,128)(2,1)S(1)}, bf16[8,128,256]{2,1,0:T(8,128)(2,1)S(1)}, u32[]{:S(2)}, u32[]{:S(2)}) %collective-permute-start.1) | collective-permute-done | bytes 524320 | tf_op jit(solution)/shard_map/ppermute | solution.py:320
  52.5 2.8 %collective-permute-done.2 = bf16[8,128,256]{2,1,0:T(8,128)(2,1)S(1)} collective-permute-done((bf16[8,128,256]{2,1,0:T(8,128)(2,1)S(1)}, bf16[8,128,256]{2,1,0:T(8,128)(2,1)S(1)}, u32[]{:S(2)}, u32[]{:S(2)}) %collective-permute-start.2) | collective-permute-done | bytes 524320 | tf_op jit(solution)/shard_map/ppermute | solution.py:320
  55.4 0.0 copy-start
  55.4 3.6 %collective-permute-start.3 = (bf16[32,128,256]{2,1,0:T(8,128)(2,1)S(1)}, bf16[32,128,256]{2,1,0:T(8,128)(2,1)}, u32[]{:S(2)}, u32[]{:S(2)}) collective-permute-start(bf16[32,128,256]{2,1,0:T(8,128)(2,1)S(1)} %constant_dynamic-update-slice_fusion.pairs_ref), channel_id=1, source_target_pairs={{0,12},{12,0},{24,36},{36,24},{48,60},{60,48},{72,84},{84,72},{96,... | collective-permute-start | bytes 6291464 | tf_op jit(solution)/shard_map/ppermute | solution.py:330
  59.0 2.1 %memory.1 = bf16[64,16,128]{2,1,0:T(8,128)(2,1)} custom-call(bf16[128,512]{1,0:T(8,128)(2,1)} %key_ref.4, bf16[128,512]{1,0:T(8,128)(2,1)} %value_ref.4, f32[4,128]{1,0:T(4,128)} %log_ref.5), custom_call_target="tpu_custom_call" | custom-call | tf_op jit(solution)/shard_map/memory/pallas_call | solution.py:222
  61.1 19.4 %all_to_all.21.in_ref = bf16[64,16,128]{2,1,0:T(8,128)(2,1)} all-to-all(bf16[64,16,128]{2,1,0:T(8,128)(2,1)} %memory.1), channel_id=1, replica_groups=mesh['seq'=64,'head'=12] {'seq'}, dimensions={0} | all-to-all | bytes 524288 | tf_op jit(solution)/shard_map/all_to_all | solution.py:323
  80.5 2.3 %scan.1 = bf16[64,8,128]{2,1,0:T(8,128)(2,1)} custom-call(bf16[64,16,128]{2,1,0:T(8,128)(2,1)} %all_to_all.21.in_ref), custom_call_target="tpu_custom_call" | custom-call | tf_op jit(solution)/shard_map/scan/pallas_call | solution.py:229
  82.7 4.8 %all-to-all-start.1 = ((bf16[64,8,128]{2,1,0:T(8,128)(2,1)}), bf16[64,8,128]{2,1,0:T(8,128)(2,1)S(1)}, u32[]{:S(2)}, u32[]{:S(2)}) async-start(bf16[64,8,128]{2,1,0:T(8,128)(2,1)} %scan.1), calls=%async_computation.1 | async-start | bytes 262144 | tf_op jit(solution)/shard_map/all_to_all | solution.py:325
  87.5 2.5 %inside.1.inside_ref = f32[128,512]{1,0:T(8,128)} custom-call(bf16[128,512]{1,0:T(8,128)(2,1)} %query_ref.5, bf16[128,512]{1,0:T(8,128)(2,1)} %key_ref.4, bf16[128,512]{1,0:T(8,128)(2,1)} %value_ref.4, f32[4,128]{1,0:T(4,128)} %log_ref.5), custom_call_target="tpu_custom_call" | custom-call | tf_op jit(solution)/shard_map/inside/pallas_call | solution.py:236
  90.0 8.6 %all-to-all-done.1.memory_ref = bf16[64,8,128]{2,1,0:T(8,128)(2,1)S(1)} async-done(((bf16[64,8,128]{2,1,0:T(8,128)(2,1)}), bf16[64,8,128]{2,1,0:T(8,128)(2,1)S(1)}, u32[]{:S(2)}, u32[]{:S(2)}) %all-to-all-start.1) | async-done | bytes 131104 | tf_op jit(solution)/shard_map/all_to_all | solution.py:325
  98.6 0.0 copy-start.1
  98.6 0.7 copy-done.1
  99.2 2.0 %mixed.1 = (f32[128,512]{1,0:T(8,128)}, f32[12,8,128]{2,1,0:T(8,128)}) custom-call(bf16[128,512]{1,0:T(8,128)(2,1)} %query_ref.5, f32[4,128]{1,0:T(4,128)} %log_ref.5, f32[128,512]{1,0:T(8,128)} %inside.1.inside_ref, bf16[64,8,128]{2,1,0:T(8,128)(2,1)} %copy-done.1), custom_call_target="tpu_custom_call" | custom-call | tf_op jit(solution)/shard_map/mixed/pallas_call | solution.py:243
  101.2 14.9 %all-to-all-start.2 = ((f32[12,8,128]{2,1,0:T(8,128)}), f32[12,8,128]{2,1,0:T(8,128)S(1)}, u32[]{:S(2)}, u32[]{:S(2)}) async-start(f32[12,8,128]{2,1,0:T(8,128)} %get-tuple-element.8), calls=%async_computation.2 | async-start | bytes 98304 | tf_op jit(solution)/shard_map/all_to_all | solution.py:328
  116.1 9.7 %all-to-all-done.2.square_ref = f32[12,8,128]{2,1,0:T(8,128)S(1)} async-done(((f32[12,8,128]{2,1,0:T(8,128)}), f32[12,8,128]{2,1,0:T(8,128)S(1)}, u32[]{:S(2)}, u32[]{:S(2)}) %all-to-all-start.2) | async-done | bytes 49184 | tf_op jit(solution)/shard_map/all_to_all | solution.py:328
  125.8 0.0 copy-start.2
  125.8 0.6 copy-done.2
  126.4 1.8 %gate.1 = bf16[128,512]{1,0:T(8,128)(2,1)} custom-call(f32[128,512]{1,0:T(8,128)} %get-tuple-element.7.mixed_ref, f32[12,8,128]{2,1,0:T(8,128)} %copy-done.2, f32[1,512]{1,0:T(1,128)} %bitcast.3, bf16[128,512]{1,0:T(8,128)(2,1)} %gate_ref.1), custom_call_target="tpu_custom_call" | custom-call | tf_op jit(solution)/shard_map/gate/pallas_call | solution.py:251
  128.2 0.0 copy-done
  128.2 10.2 %attend_first.1 = (f32[4,128,128]{2,1,0:T(8,128)}, f32[4,128,128]{2,1,0:T(8,128)}, f32[4,128,128]{2,1,0:T(8,128)}) custom-call(s32[64]{0:T(128)} %seg_ref.3, s32[1]{0:T(128)} %bitcast.1.place_ref, bf16[128,512]{1,0:T(8,128)(2,1)} %query_ref.7, bf16[8,128,256]{2,1,0:T(8,128)(2,1)} %pieces.1.own_ref, bf16[32,128,256]{2,1,0:T(8,128)(2,1)} %copy-done), custom_call_target="tpu_custom_call" | custom-call | tf_op jit(solution)/shard_map/attend_first/pallas_call | solution.py:274
  138.4 0.0 collective-permute-done.3.pairs_ref
  138.4 10.2 %attend_second.1 = bf16[128,512]{1,0:T(8,128)(2,1)} custom-call(s32[64]{0:T(128)} %seg_ref.3, s32[1]{0:T(128)} %bitcast.1.place_ref, bf16[128,512]{1,0:T(8,128)(2,1)} %query_ref.7, bf16[32,128,256]{2,1,0:T(8,128)(2,1)} %collective-permute-done.3.pairs_ref, f32[4,128,128]{2,1,0:T(8,128)} %get-tuple-element.9.acc_ref, ...), custom_call_target="tpu_custom_call" | custom-call | tf_op jit(solution)/shard_map/attend_second/pallas_call | solution.py:289
  (4 shorter events, 0.1 us)
Async XLA Ops:
  22.2 16.7 %collective-permute-start = (bf16[8,128,256]{2,1,0:T(8,128)(2,1)S(1)}, bf16[8,128,256]{2,1,0:T(8,128)(2,1)S(1)}, u32[]{:S(2)}, u32[]{:S(2)}) collective-permute-start(bf16[8,128,256]{2,1,0:T(8,128)(2,1)S(1)} %all_to_all.20), channel_id=1, source_target_pairs={{0,24},{12,36},{24,48},{36,60},{48,72},{60,84},{72,0},{84,12},{96,... | collective-permute-start | bytes 1572872 | tf_op jit(solution)/shard_map/ppermute | solution.py:320
  29.2 23.3 %collective-permute-start.1 = (bf16[8,128,256]{2,1,0:T(8,128)(2,1)S(1)}, bf16[8,128,256]{2,1,0:T(8,128)(2,1)S(1)}, u32[]{:S(2)}, u32[]{:S(2)}) collective-permute-start(bf16[8,128,256]{2,1,0:T(8,128)(2,1)S(1)} %all_to_all.20), channel_id=1, source_target_pairs={{0,48},{12,60},{24,72},{36,84},{48,0},{60,12},{72,24},{84,36},{96,... | collective-permute-start | bytes 1572872 | tf_op jit(solution)/shard_map/ppermute | solution.py:320
  33.5 21.9 %collective-permute-start.2 = (bf16[8,128,256]{2,1,0:T(8,128)(2,1)S(1)}, bf16[8,128,256]{2,1,0:T(8,128)(2,1)S(1)}, u32[]{:S(2)}, u32[]{:S(2)}) collective-permute-start(bf16[8,128,256]{2,1,0:T(8,128)(2,1)S(1)} %all_to_all.20), channel_id=1, source_target_pairs={{0,72},{12,84},{24,0},{36,12},{48,24},{60,36},{72,48},{84,60},{96,... | collective-permute-start | bytes 1572872 | tf_op jit(solution)/shard_map/ppermute | solution.py:320
  55.4 72.8 %copy-start = (bf16[32,128,256]{2,1,0:T(8,128)(2,1)}, bf16[32,128,256]{2,1,0:T(8,128)(2,1)S(1)}, u32[]{:S(2)}) copy-start(bf16[32,128,256]{2,1,0:T(8,128)(2,1)S(1)} %constant_dynamic-update-slice_fusion.pairs_ref) | copy-start | bytes 6291460
  55.4 83.0 %collective-permute-start.3 = (bf16[32,128,256]{2,1,0:T(8,128)(2,1)S(1)}, bf16[32,128,256]{2,1,0:T(8,128)(2,1)}, u32[]{:S(2)}, u32[]{:S(2)}) collective-permute-start(bf16[32,128,256]{2,1,0:T(8,128)(2,1)S(1)} %constant_dynamic-update-slice_fusion.pairs_ref), channel_id=1, source_target_pairs={{0,12},{12,0},{24,36},{36,24},{48,60},{60,48},{72,84},{84,72},{96,... | collective-permute-start | bytes 6291464 | tf_op jit(solution)/shard_map/ppermute | solution.py:330
  82.7 15.9 %all-to-all-start.1 = ((bf16[64,8,128]{2,1,0:T(8,128)(2,1)}), bf16[64,8,128]{2,1,0:T(8,128)(2,1)S(1)}, u32[]{:S(2)}, u32[]{:S(2)}) async-start(bf16[64,8,128]{2,1,0:T(8,128)(2,1)} %scan.1), calls=%async_computation.1 | async-start | bytes 262144 | tf_op jit(solution)/shard_map/all_to_all | solution.py:325
  98.6 0.7 copy-start.1
  101.2 24.6 %all-to-all-start.2 = ((f32[12,8,128]{2,1,0:T(8,128)}), f32[12,8,128]{2,1,0:T(8,128)S(1)}, u32[]{:S(2)}, u32[]{:S(2)}) async-start(f32[12,8,128]{2,1,0:T(8,128)} %get-tuple-element.8), calls=%async_computation.2 | async-start | bytes 98304 | tf_op jit(solution)/shard_map/all_to_all | solution.py:328
  125.8 0.6 copy-start.2

commit v2 on v1

--- a/solution.py
+++ b/solution.py
@@ -11,10 +11,8 @@
 Q_PER_KV = 8
 TOK = 128
 SEGS = 64
-HALF = 32
 ROWS = 8
 COLUMNS = 4
-KEY_BLOCK = 8
 
 norm_eps = 1e-06
 SCALE = HEAD_DIM ** (-0.5)
@@ -142,76 +140,114 @@
     out_ref[:, :, HEAD_DIM:] = jnp.broadcast_to(value_ref[...][None], (ROWS, TOK, HEAD_DIM))
 
 
-def attend(place, core, seg_ref, own_segment, query_ref, pairs_ref, state):
-    def block(step, state):
-        column = jnp.bitwise_and(place // 2 - step, COLUMNS - 1)
-        rows = pairs_ref[pl.ds(step * KEY_BLOCK, KEY_BLOCK)]
-        keys = rows[:, :, 0:HEAD_DIM].reshape(KEY_BLOCK * TOK, HEAD_DIM)
-        values = rows[:, :, HEAD_DIM:].reshape(KEY_BLOCK * TOK, HEAD_DIM)
-        shift = []
-        for at in range(KEY_BLOCK):
-            seg = seg_ref[at * ROWS + column * 2 + core]
-            shift.append(jnp.where(seg < own_segment, 0.0, MASKED).astype(F32))
-        new_state = []
-        for head in range(HEADS_DEV):
-            peak, total, acc = state[head]
-            query = query_ref[:, head * HEAD_DIM : (head + 1) * HEAD_DIM]
-            logits = dot(query, keys, 1, 1)
-            parts = [logits[:, at * TOK : (at + 1) * TOK] + shift[at] for at in range(KEY_BLOCK)]
-            top = parts[0]
-            for part in parts[1:]:
-                top = jnp.maximum(top, part)
-            new_peak = jnp.maximum(peak, jnp.max(top, axis=1, keepdims=True))
-            fade = jnp.exp2((peak - new_peak) * (SCALE * LOG2E))
-            weights = [jnp.exp2((part - new_peak) * (SCALE * LOG2E)) for part in parts]
-            summed = weights[0]
-            for part in weights[1:]:
-                summed = summed + part
-            low = jnp.concatenate([part.astype(BF16) for part in weights], axis=1)
-            new_state.append(
-                (new_peak, total * fade + summed, acc * fade + dot(low, values, 1, 0))
-            )
-        return tuple(new_state)
-
-    return lax.fori_loop(0, HALF // KEY_BLOCK, block, state)
-
-
-def first_kernel(
-    seg_ref, place_ref, query_ref, own_ref, pairs_ref, acc_ref, total_ref, peak_ref
+def stack_heads(query_ref, heads_ref):
+    for head in range(HEADS_DEV):
+        heads_ref[head * TOK : (head + 1) * TOK] = query_ref[:, head * HEAD_DIM : (head + 1) * HEAD_DIM]
+
+
+def score_columns(pairs_ref, columns, core, place, seg_ref, heads_ref, score_ref, top_ref):
+    own_segment = seg_ref[place]
+
+    def score(column, carry):
+        source = jnp.bitwise_and(place // 2 - column, COLUMNS - 1)
+        keys = pairs_ref[pl.ds(column * ROWS, ROWS), :, 0:HEAD_DIM].reshape(ROWS * TOK, HEAD_DIM)
+        logits = dot(heads_ref[...], keys, 1, 1)
+        top = top_ref[...]
+        for at in range(ROWS):
+            seg = seg_ref[at * ROWS + source * 2 + core]
+            part = logits[:, at * TOK : (at + 1) * TOK] + jnp.where(seg < own_segment, 0.0, MASKED).astype(F32)
+            top = jnp.maximum(top, part)
+            score_ref[column - columns[0], :, at * TOK : (at + 1) * TOK] = part
+        top_ref[...] = top
+        return carry
+
+    lax.fori_loop(*columns, score, 0)
+
+
+def weigh_columns(pairs_ref, columns, score_ref, peak_ref, total_ref, acc_ref):
+    def weigh(column, carry):
+        values = pairs_ref[pl.ds(column * ROWS, ROWS), :, HEAD_DIM:].reshape(ROWS * TOK, HEAD_DIM)
+        peak = peak_ref[...]
+        total = total_ref[...]
+        low = []
+        for at in range(ROWS):
+            part = score_ref[column - columns[0], :, at * TOK : (at + 1) * TOK]
+            weights = jnp.exp2((part - peak) * (SCALE * LOG2E))
+            total = total + weights
+            low.append(weights.astype(BF16))
+        total_ref[...] = total
+        acc_ref[...] += dot(jnp.concatenate(low, axis=1), values, 1, 0)
+        return carry
+
+    lax.fori_loop(*columns, weigh, 0)
+
+
+def widest(top):
+    return jnp.broadcast_to(jnp.max(top, axis=1, keepdims=True), top.shape)
+
+
+def own_kernel(
+    seg_ref, place_ref, query_ref, own_ref, column_ref,
+    peak_ref, total_ref, acc_ref, heads_ref, score_ref, own_score_ref,
 ):
     place = place_ref[0]
-    own_segment = seg_ref[place]
-    row, col = iotas()
-    keys = own_ref[0, :, 0:HEAD_DIM]
-    values = own_ref[0, :, HEAD_DIM:]
-    state = []
-    for head in range(HEADS_DEV):
-        query = query_ref[:, head * HEAD_DIM : (head + 1) * HEAD_DIM]
-        logits = jnp.where(col <= row, dot(query, keys, 1, 1), MASKED)
-        peak = jnp.max(logits, axis=1, keepdims=True)
-        weights = jnp.exp2((logits - peak) * (SCALE * LOG2E))
-        state.append((peak, weights, dot(weights.astype(BF16), values, 1, 0)))
-    state = attend(place, place % 2, seg_ref, own_segment, query_ref, pairs_ref, tuple(state))
-    for head in range(HEADS_DEV):
-        peak, total, acc = state[head]
-        acc_ref[head] = acc
-        total_ref[head] = total
-        peak_ref[head] = jnp.broadcast_to(peak, (TOK, HEAD_DIM))
-
-
-def second_kernel(
-    seg_ref, place_ref, query_ref, pairs_ref, acc_ref, total_ref, peak_ref, out_ref
+    stack_heads(query_ref, heads_ref)
+    row = jnp.bitwise_and(lax.broadcasted_iota(jnp.int32, (HEADS_DEV * TOK, TOK), 0), TOK - 1)
+    col = lax.broadcasted_iota(jnp.int32, (HEADS_DEV * TOK, TOK), 1)
+    logits = jnp.where(col <= row, dot(heads_ref[...], own_ref[0, :, 0:HEAD_DIM], 1, 1), MASKED)
+    own_score_ref[...] = logits
+    peak_ref[...] = logits
+    score_columns(column_ref, (0, 1), place % 2, place, seg_ref, heads_ref, score_ref, peak_ref)
+    peak_ref[...] = widest(peak_ref[...])
+    weights = jnp.exp2((own_score_ref[...] - peak_ref[...]) * (SCALE * LOG2E))
+    total_ref[...] = weights
+    acc_ref[...] = dot(weights.astype(BF16), own_ref[0, :, HEAD_DIM:], 1, 0)
+    weigh_columns(column_ref, (0, 1), score_ref, peak_ref, total_ref, acc_ref)
+
+
+def later_columns(pairs_ref, columns, core, seg_ref, place, query_ref, old, new, scratch):
+    heads_ref, score_ref = scratch
+    old_peak_ref, old_total_ref, old_acc_ref = old
+    peak_ref, total_ref, acc_ref = new
+    stack_heads(query_ref, heads_ref)
+    peak_ref[...] = old_peak_ref[...]
+    score_columns(pairs_ref, columns, core, place, seg_ref, heads_ref, score_ref, peak_ref)
+    peak = widest(peak_ref[...])
+    peak_ref[...] = peak
+    fade = jnp.exp2((old_peak_ref[...] - peak) * (SCALE * LOG2E))
+    total_ref[...] = old_total_ref[...] * fade
+    acc_ref[...] = old_acc_ref[...] * fade
+    weigh_columns(pairs_ref, columns, score_ref, peak_ref, total_ref, acc_ref)
+
+
+def shifted_kernel(
+    seg_ref, place_ref, query_ref, pairs_ref,
+    old_peak_ref, old_total_ref, old_acc_ref,
+    peak_ref, total_ref, acc_ref, heads_ref, score_ref,
 ):
     place = place_ref[0]
-    own_segment = seg_ref[place]
-    state = tuple(
-        (peak_ref[head][:, 0:1], total_ref[head], acc_ref[head]) for head in range(HEADS_DEV)
-    )
-    state = attend(place, 1 - place % 2, seg_ref, own_segment, query_ref, pairs_ref, state)
+    later_columns(
+        pairs_ref, (1, COLUMNS), place % 2, seg_ref, place, query_ref,
+        (old_peak_ref, old_total_ref, old_acc_ref), (peak_ref, total_ref, acc_ref),
+        (heads_ref, score_ref),
+    )
+
+
+def swapped_kernel(
+    seg_ref, place_ref, query_ref, pairs_ref,
+    old_peak_ref, old_total_ref, old_acc_ref,
+    out_ref, peak_ref, total_ref, acc_ref, heads_ref, score_ref,
+):
+    place = place_ref[0]
+    later_columns(
+        pairs_ref, (0, COLUMNS), 1 - place % 2, seg_ref, place, query_ref,
+        (old_peak_ref, old_total_ref, old_acc_ref), (peak_ref, total_ref, acc_ref),
+        (heads_ref, score_ref),
+    )
     for head in range(HEADS_DEV):
-        _, total, acc = state[head]
-        lanes = slice(head * HEAD_DIM, (head + 1) * HEAD_DIM)
-        out_ref[:, lanes] = (acc / jnp.sum(total, axis=1, keepdims=True)).astype(BF16)
+        rows = slice(head * TOK, (head + 1) * TOK)
+        total = jnp.sum(total_ref[rows], axis=1, keepdims=True)
+        out_ref[:, head * HEAD_DIM : (head + 1) * HEAD_DIM] = (acc_ref[rows] / total).astype(BF16)
 
 
 def shape(*dims, dtype=F32):
@@ -270,26 +306,50 @@
     )(place, key, value)
 
 
-def attend_first(segment_of, place, query, pieces, pairs):
-    return pl.pallas_call(
-        first_kernel, name="attend_first",
-        out_shape=(shape(HEADS_DEV, TOK, HEAD_DIM),) * 3,
+STACKED = HEADS_DEV * TOK
+
+
+def state_scratch(count):
+    return [pltpu.VMEM((STACKED, HEAD_DIM), F32)] * count
+
+
+def score_scratch(columns):
+    return [
+        pltpu.VMEM((STACKED, HEAD_DIM), BF16),
+        pltpu.VMEM((columns, STACKED, ROWS * TOK), F32),
+    ]
+
+
+def attend_own(segment_of, place, query, pieces, column):
+    whole = lambda *dims: pl.BlockSpec(dims, lambda i: (0,) * len(dims))
+    return pl.pallas_call(
+        own_kernel, name="own",
+        out_shape=(shape(STACKED, HEAD_DIM),) * 3,
         grid=(1,),
         in_specs=[
-            SM, SM,
-            pl.BlockSpec((TOK, HEADS_DEV * HEAD_DIM), lambda i: (0, 0)),
-            pl.BlockSpec((1, TOK, 2 * HEAD_DIM), lambda i: (0, 0, 0)),
-            pl.BlockSpec((HALF, TOK, 2 * HEAD_DIM), lambda i: (0, 0, 0)),
+            SM, SM, whole(TOK, HEADS_DEV * HEAD_DIM), whole(1, TOK, 2 * HEAD_DIM),
+            whole(ROWS, TOK, 2 * HEAD_DIM),
         ],
-        out_specs=(pl.BlockSpec((HEADS_DEV, TOK, HEAD_DIM), lambda i: (0, 0, 0)),) * 3,
-    )(segment_of, place, query, pieces, pairs)
-
-
-def attend_second(segment_of, place, query, pairs, state):
-    return pl.pallas_call(
-        second_kernel, name="attend_second",
+        out_specs=(whole(STACKED, HEAD_DIM),) * 3,
+        scratch_shapes=score_scratch(1) + state_scratch(1),
+    )(segment_of, place, query, pieces, column)
+
+
+def attend_shifted(segment_of, place, query, pairs, state):
+    return pl.pallas_call(
+        shifted_kernel, name="shifted",
+        out_shape=(shape(STACKED, HEAD_DIM),) * 3,
+        in_specs=[SM, SM] + [VM] * 5, out_specs=(VM,) * 3,
+        scratch_shapes=score_scratch(COLUMNS - 1),
+    )(segment_of, place, query, pairs, *state)
+
+
+def attend_swapped(segment_of, place, query, pairs, state):
+    return pl.pallas_call(
+        swapped_kernel, name="swapped",
         out_shape=shape(TOK, HEADS_DEV * HEAD_DIM, dtype=BF16),
         in_specs=[SM, SM] + [VM] * 5, out_specs=VM,
+        scratch_shapes=state_scratch(3) + score_scratch(COLUMNS),
     )(segment_of, place, query, pairs, *state)
 
 
@@ -328,8 +388,9 @@
     squares = lax.all_to_all(squares, "head", 0, 0, tiled=True)
     lin_out = gate_part(mixed, squares, norm_gain, out_gate)
     others = lax.ppermute(pairs, "seq", partners)
-    state = attend_first(segment_of, place, soft_query, pieces, pairs)
-    soft_out = attend_second(segment_of, place, soft_query, others, state)
+    state = attend_own(segment_of, place, soft_query, pieces, column)
+    state = attend_shifted(segment_of, place, soft_query, pairs, state)
+    soft_out = attend_swapped(segment_of, place, soft_query, others, state)
     return (lin_out, soft_out)
 
 

time: 149 us -> 144 us (0.966)
  Pallas kernels: 32.6 us -> 27.5 us
    pallas_call x2 -> x3, Pallas kernels: 20.4 us -> 15.3 us  [the longest x1 6.51 us: attend_swapped(): pl.pallas_call(swapped_kernel, name='swapped', out_shape=shape(TOK, HEADS...]
where the time goes in v2:
time: 144 us
  blocking collectives  39.2 us (27%)
  starting transfers between devices  37.6 us (26%)
  waiting for transfers between devices  36.9 us (26%)
  Pallas kernels  27.5 us (19%)
    all_to_all x1, blocking collectives, shards(): lax.all_to_all(pieces, 'seq', 0, 0, tiled=True, axis_index_groups=same_co...  19.9 us
    all_to_all x1, blocking collectives, shards(): received = lax.all_to_all(local, 'seq', 0, 0, tiled=True)  19.4 us
    ppermute x3, waiting for transfers between devices, shards(): lax.ppermute(column, 'seq', shifts[step])  18.7 us
    all_to_all x1, starting transfers between devices, shards(): squares = lax.all_to_all(squares, 'head', 0, 0, tiled=True)  14.9 us
    ppermute x3, starting transfers between devices, shards(): lax.ppermute(column, 'seq', shifts[step])  14.4 us
    all_to_all x1, waiting for transfers between devices, shards(): squares = lax.all_to_all(squares, 'head', 0, 0, tiled=True)  9.68 us
    all_to_all x1, waiting for transfers between devices, shards(): memory = lax.all_to_all(scanned, 'seq', 0, 0, tiled=True)  8.6 us
    pallas_call x1, Pallas kernels, attend_swapped(): pl.pallas_call(swapped_kernel, name='swapped', out_shape=shape(TOK, HEADS...  6.51 us
  transfers between devices with their start and end apart: 6, of which 5 were waited for; matrix products, arithmetic and copies ran while one was open for 0% of the time, Pallas kernels for 14%

profile of v2, /device:TPU:1, one launch (start us, length us, event | category | flops | bytes accessed | tf_op | source)
XLA Modules:
  0.0 143.5 jit_solution(2690605037011686818)
XLA Ops:
  0.7 1.6 %pieces.1.own_ref = bf16[8,128,256]{2,1,0:T(8,128)(2,1)} custom-call(s32[1]{0:T(128)} %bitcast.2.place_ref, bf16[128,768]{1,0:T(8,128)(2,1)} %key_ref.5, bf16[128,768]{1,0:T(8,128)(2,1)} %value_ref.5), custom_call_target="tpu_custom_call" | custom-call | tf_op jit(solution)/shard_map/pieces/pallas_call | solution.py:294
  2.3 19.9 %all_to_all.20.column_ref = bf16[8,128,256]{2,1,0:T(8,128)(2,1)S(1)} all-to-all(bf16[8,128,256]{2,1,0:T(8,128)(2,1)} %pieces.1.own_ref), channel_id=1, replica_groups={{0,96,192,288,384,480,576,672},{12,108,204,300,396,492,588,684},{24,120..., dimensions={0} | all-to-all | bytes 1048576 | tf_op jit(solution)/shard_map/all_to_all | solution.py:377
  22.2 0.0 copy-start
  22.2 7.0 %collective-permute-start = (bf16[8,128,256]{2,1,0:T(8,128)(2,1)S(1)}, bf16[8,128,256]{2,1,0:T(8,128)(2,1)S(1)}, u32[]{:S(2)}, u32[]{:S(2)}) collective-permute-start(bf16[8,128,256]{2,1,0:T(8,128)(2,1)S(1)} %all_to_all.20.column_ref), channel_id=1, source_target_pairs={{0,24},{12,36},{24,48},{36,60},{48,72},{60,84},{72,0},{84,12},{96,... | collective-permute-start | bytes 1572872 | tf_op jit(solution)/shard_map/ppermute | solution.py:380
  29.2 4.4 %collective-permute-start.1 = (bf16[8,128,256]{2,1,0:T(8,128)(2,1)S(1)}, bf16[8,128,256]{2,1,0:T(8,128)(2,1)S(1)}, u32[]{:S(2)}, u32[]{:S(2)}) collective-permute-start(bf16[8,128,256]{2,1,0:T(8,128)(2,1)S(1)} %all_to_all.20.column_ref), channel_id=1, source_target_pairs={{0,48},{12,60},{24,72},{36,84},{48,0},{60,12},{72,24},{84,36},{96,... | collective-permute-start | bytes 1572872 | tf_op jit(solution)/shard_map/ppermute | solution.py:380
  33.5 3.1 %collective-permute-start.2 = (bf16[8,128,256]{2,1,0:T(8,128)(2,1)S(1)}, bf16[8,128,256]{2,1,0:T(8,128)(2,1)S(1)}, u32[]{:S(2)}, u32[]{:S(2)}) collective-permute-start(bf16[8,128,256]{2,1,0:T(8,128)(2,1)S(1)} %all_to_all.20.column_ref), channel_id=1, source_target_pairs={{0,72},{12,84},{24,0},{36,12},{48,24},{60,36},{72,48},{84,60},{96,... | collective-permute-start | bytes 1572872 | tf_op jit(solution)/shard_map/ppermute | solution.py:380
  36.7 2.2 %collective-permute-done = bf16[8,128,256]{2,1,0:T(8,128)(2,1)S(1)} collective-permute-done((bf16[8,128,256]{2,1,0:T(8,128)(2,1)S(1)}, bf16[8,128,256]{2,1,0:T(8,128)(2,1)S(1)}, u32[]{:S(2)}, u32[]{:S(2)}) %collective-permute-start) | collective-permute-done | bytes 524320 | tf_op jit(solution)/shard_map/ppermute | solution.py:380
  38.9 13.6 %collective-permute-done.1 = bf16[8,128,256]{2,1,0:T(8,128)(2,1)S(1)} collective-permute-done((bf16[8,128,256]{2,1,0:T(8,128)(2,1)S(1)}, bf16[8,128,256]{2,1,0:T(8,128)(2,1)S(1)}, u32[]{:S(2)}, u32[]{:S(2)}) %collective-permute-start.1) | collective-permute-done | bytes 524320 | tf_op jit(solution)/shard_map/ppermute | solution.py:380
  52.6 2.8 %collective-permute-done.2 = bf16[8,128,256]{2,1,0:T(8,128)(2,1)S(1)} collective-permute-done((bf16[8,128,256]{2,1,0:T(8,128)(2,1)S(1)}, bf16[8,128,256]{2,1,0:T(8,128)(2,1)S(1)}, u32[]{:S(2)}, u32[]{:S(2)}) %collective-permute-start.2) | collective-permute-done | bytes 524320 | tf_op jit(solution)/shard_map/ppermute | solution.py:380
  55.4 0.0 copy-start.1
  55.4 3.6 %collective-permute-start.3 = (bf16[32,128,256]{2,1,0:T(8,128)(2,1)S(1)}, bf16[32,128,256]{2,1,0:T(8,128)(2,1)}, u32[]{:S(2)}, u32[]{:S(2)}) collective-permute-start(bf16[32,128,256]{2,1,0:T(8,128)(2,1)S(1)} %constant_dynamic-update-slice_fusion.pairs_ref), channel_id=1, source_target_pairs={{0,12},{12,0},{24,36},{36,24},{48,60},{60,48},{72,84},{84,72},{96,... | collective-permute-start | bytes 6291464 | tf_op jit(solution)/shard_map/ppermute | solution.py:390
  59.0 2.1 %memory.1 = bf16[64,16,128]{2,1,0:T(8,128)(2,1)} custom-call(bf16[128,512]{1,0:T(8,128)(2,1)} %key_ref.4, bf16[128,512]{1,0:T(8,128)(2,1)} %value_ref.4, f32[4,128]{1,0:T(4,128)} %log_ref.5), custom_call_target="tpu_custom_call" | custom-call | tf_op jit(solution)/shard_map/memory/pallas_call | solution.py:258
  61.1 0.0 copy-done
  61.1 19.4 %all_to_all.21.in_ref = bf16[64,16,128]{2,1,0:T(8,128)(2,1)} all-to-all(bf16[64,16,128]{2,1,0:T(8,128)(2,1)} %memory.1), channel_id=1, replica_groups=mesh['seq'=64,'head'=12] {'seq'}, dimensions={0} | all-to-all | bytes 524288 | tf_op jit(solution)/shard_map/all_to_all | solution.py:383
  80.5 2.3 %scan.1 = bf16[64,8,128]{2,1,0:T(8,128)(2,1)} custom-call(bf16[64,16,128]{2,1,0:T(8,128)(2,1)} %all_to_all.21.in_ref), custom_call_target="tpu_custom_call" | custom-call | tf_op jit(solution)/shard_map/scan/pallas_call | solution.py:265
  82.7 4.8 %all-to-all-start.1 = ((bf16[64,8,128]{2,1,0:T(8,128)(2,1)}), bf16[64,8,128]{2,1,0:T(8,128)(2,1)S(1)}, u32[]{:S(2)}, u32[]{:S(2)}) async-start(bf16[64,8,128]{2,1,0:T(8,128)(2,1)} %scan.1), calls=%async_computation.1 | async-start | bytes 262144 | tf_op jit(solution)/shard_map/all_to_all | solution.py:385
  87.5 2.5 %inside.1.inside_ref = f32[128,512]{1,0:T(8,128)} custom-call(bf16[128,512]{1,0:T(8,128)(2,1)} %query_ref.6, bf16[128,512]{1,0:T(8,128)(2,1)} %key_ref.4, bf16[128,512]{1,0:T(8,128)(2,1)} %value_ref.4, f32[4,128]{1,0:T(4,128)} %log_ref.5), custom_call_target="tpu_custom_call" | custom-call | tf_op jit(solution)/shard_map/inside/pallas_call | solution.py:272
  90.0 8.6 %all-to-all-done.1.memory_ref = bf16[64,8,128]{2,1,0:T(8,128)(2,1)S(1)} async-done(((bf16[64,8,128]{2,1,0:T(8,128)(2,1)}), bf16[64,8,128]{2,1,0:T(8,128)(2,1)S(1)}, u32[]{:S(2)}, u32[]{:S(2)}) %all-to-all-start.1) | async-done | bytes 131104 | tf_op jit(solution)/shard_map/all_to_all | solution.py:385
  98.6 0.0 copy-start.2
  98.6 0.7 copy-done.2
  99.3 2.0 %mixed.1 = (f32[128,512]{1,0:T(8,128)}, f32[12,8,128]{2,1,0:T(8,128)}) custom-call(bf16[128,512]{1,0:T(8,128)(2,1)} %query_ref.6, f32[4,128]{1,0:T(4,128)} %log_ref.5, f32[128,512]{1,0:T(8,128)} %inside.1.inside_ref, bf16[64,8,128]{2,1,0:T(8,128)(2,1)} %copy-done.2), custom_call_target="tpu_custom_call" | custom-call | tf_op jit(solution)/shard_map/mixed/pallas_call | solution.py:279
  101.2 14.9 %all-to-all-start.2 = ((f32[12,8,128]{2,1,0:T(8,128)}), f32[12,8,128]{2,1,0:T(8,128)S(1)}, u32[]{:S(2)}, u32[]{:S(2)}) async-start(f32[12,8,128]{2,1,0:T(8,128)} %get-tuple-element.11), calls=%async_computation.2 | async-start | bytes 98304 | tf_op jit(solution)/shard_map/all_to_all | solution.py:388
  116.1 9.7 %all-to-all-done.2.square_ref = f32[12,8,128]{2,1,0:T(8,128)S(1)} async-done(((f32[12,8,128]{2,1,0:T(8,128)}), f32[12,8,128]{2,1,0:T(8,128)S(1)}, u32[]{:S(2)}, u32[]{:S(2)}) %all-to-all-start.2) | async-done | bytes 49184 | tf_op jit(solution)/shard_map/all_to_all | solution.py:388
  125.8 0.0 copy-start.3
  125.8 0.6 copy-done.3
  126.4 1.8 %gate.1 = bf16[128,512]{1,0:T(8,128)(2,1)} custom-call(f32[128,512]{1,0:T(8,128)} %get-tuple-element.10.mixed_ref, f32[12,8,128]{2,1,0:T(8,128)} %copy-done.3, f32[1,512]{1,0:T(1,128)} %bitcast.3, bf16[128,512]{1,0:T(8,128)(2,1)} %gate_ref.1), custom_call_target="tpu_custom_call" | custom-call | tf_op jit(solution)/shard_map/gate/pallas_call | solution.py:287
  128.2 3.3 %own.1 = (f32[512,128]{1,0:T(8,128)}, f32[512,128]{1,0:T(8,128)}, f32[512,128]{1,0:T(8,128)}) custom-call(s32[64]{0:T(128)} %seg_ref.5, s32[1]{0:T(128)} %bitcast.1.place_ref, bf16[128,512]{1,0:T(8,128)(2,1)} %query_ref.9, bf16[8,128,256]{2,1,0:T(8,128)(2,1)} %pieces.1.own_ref, bf16[8,128,256]{2,1,0:T(8,128)(2,1)} %copy-done), custom_call_target="tpu_custom_call" | custom-call | tf_op jit(solution)/shard_map/own/pallas_call | solution.py:325
  131.5 0.0 copy-done.1
  131.5 5.5 %shifted.1 = (f32[512,128]{1,0:T(8,128)}, f32[512,128]{1,0:T(8,128)}, f32[512,128]{1,0:T(8,128)}) custom-call(s32[64]{0:T(128)} %seg_ref.5, s32[1]{0:T(128)} %bitcast.1.place_ref, bf16[128,512]{1,0:T(8,128)(2,1)} %query_ref.9, bf16[32,128,256]{2,1,0:T(8,128)(2,1)} %copy-done.1, f32[512,128]{1,0:T(8,128)} %get-tuple-element.12.old_peak_ref, ...), custom_call_target="tpu_custom_call" | custom-call | tf_op jit(solution)/shard_map/shifted/pallas_call | solution.py:339
  137.0 0.0 collective-permute-done.3.pairs_ref
  137.0 6.5 %swapped.1 = bf16[128,512]{1,0:T(8,128)(2,1)} custom-call(s32[64]{0:T(128)} %seg_ref.5, s32[1]{0:T(128)} %bitcast.1.place_ref, bf16[128,512]{1,0:T(8,128)(2,1)} %query_ref.9, bf16[32,128,256]{2,1,0:T(8,128)(2,1)} %collective-permute-done.3.pairs_ref, f32[512,128]{1,0:T(8,128)} %get-tuple-element.15.old_peak_ref, f32[512,128]{1,0:T(8,128)} %get-tuple-element.16.old_total_ref, ...), custom_call_target="tpu_custom_call" | custom-call | tf_op jit(solution)/shard_map/swapped/pallas_call | solution.py:348
  (4 shorter events, 0.1 us)
Async XLA Ops:
  22.2 38.9 %copy-start = (bf16[8,128,256]{2,1,0:T(8,128)(2,1)}, bf16[8,128,256]{2,1,0:T(8,128)(2,1)S(1)}, u32[]{:S(2)}) copy-start(bf16[8,128,256]{2,1,0:T(8,128)(2,1)S(1)} %all_to_all.20.column_ref) | copy-start | bytes 1572868
  22.2 16.7 %collective-permute-start = (bf16[8,128,256]{2,1,0:T(8,128)(2,1)S(1)}, bf16[8,128,256]{2,1,0:T(8,128)(2,1)S(1)}, u32[]{:S(2)}, u32[]{:S(2)}) collective-permute-start(bf16[8,128,256]{2,1,0:T(8,128)(2,1)S(1)} %all_to_all.20.column_ref), channel_id=1, source_target_pairs={{0,24},{12,36},{24,48},{36,60},{48,72},{60,84},{72,0},{84,12},{96,... | collective-permute-start | bytes 1572872 | tf_op jit(solution)/shard_map/ppermute | solution.py:380
  29.2 23.3 %collective-permute-start.1 = (bf16[8,128,256]{2,1,0:T(8,128)(2,1)S(1)}, bf16[8,128,256]{2,1,0:T(8,128)(2,1)S(1)}, u32[]{:S(2)}, u32[]{:S(2)}) collective-permute-start(bf16[8,128,256]{2,1,0:T(8,128)(2,1)S(1)} %all_to_all.20.column_ref), channel_id=1, source_target_pairs={{0,48},{12,60},{24,72},{36,84},{48,0},{60,12},{72,24},{84,36},{96,... | collective-permute-start | bytes 1572872 | tf_op jit(solution)/shard_map/ppermute | solution.py:380
  33.5 21.9 %collective-permute-start.2 = (bf16[8,128,256]{2,1,0:T(8,128)(2,1)S(1)}, bf16[8,128,256]{2,1,0:T(8,128)(2,1)S(1)}, u32[]{:S(2)}, u32[]{:S(2)}) collective-permute-start(bf16[8,128,256]{2,1,0:T(8,128)(2,1)S(1)} %all_to_all.20.column_ref), channel_id=1, source_target_pairs={{0,72},{12,84},{24,0},{36,12},{48,24},{60,36},{72,48},{84,60},{96,... | collective-permute-start | bytes 1572872 | tf_op jit(solution)/shard_map/ppermute | solution.py:380
  55.4 76.1 %copy-start.1 = (bf16[32,128,256]{2,1,0:T(8,128)(2,1)}, bf16[32,128,256]{2,1,0:T(8,128)(2,1)S(1)}, u32[]{:S(2)}) copy-start(bf16[32,128,256]{2,1,0:T(8,128)(2,1)S(1)} %constant_dynamic-update-slice_fusion.pairs_ref) | copy-start | bytes 6291460
  55.4 81.6 %collective-permute-start.3 = (bf16[32,128,256]{2,1,0:T(8,128)(2,1)S(1)}, bf16[32,128,256]{2,1,0:T(8,128)(2,1)}, u32[]{:S(2)}, u32[]{:S(2)}) collective-permute-start(bf16[32,128,256]{2,1,0:T(8,128)(2,1)S(1)} %constant_dynamic-update-slice_fusion.pairs_ref), channel_id=1, source_target_pairs={{0,12},{12,0},{24,36},{36,24},{48,60},{60,48},{72,84},{84,72},{96,... | collective-permute-start | bytes 6291464 | tf_op jit(solution)/shard_map/ppermute | solution.py:390
  82.7 15.9 %all-to-all-start.1 = ((bf16[64,8,128]{2,1,0:T(8,128)(2,1)}), bf16[64,8,128]{2,1,0:T(8,128)(2,1)S(1)}, u32[]{:S(2)}, u32[]{:S(2)}) async-start(bf16[64,8,128]{2,1,0:T(8,128)(2,1)} %scan.1), calls=%async_computation.1 | async-start | bytes 262144 | tf_op jit(solution)/shard_map/all_to_all | solution.py:385
  98.6 0.7 copy-start.2
  101.2 24.6 %all-to-all-start.2 = ((f32[12,8,128]{2,1,0:T(8,128)}), f32[12,8,128]{2,1,0:T(8,128)S(1)}, u32[]{:S(2)}, u32[]{:S(2)}) async-start(f32[12,8,128]{2,1,0:T(8,128)} %get-tuple-element.11), calls=%async_computation.2 | async-start | bytes 98304 | tf_op jit(solution)/shard_map/all_to_all | solution.py:388
  125.8 0.6 copy-start.3

commit v3 on v2

--- a/solution.py
+++ b/solution.py
@@ -11,6 +11,7 @@
 Q_PER_KV = 8
 TOK = 128
 SEGS = 64
+HALF = 32
 ROWS = 8
 COLUMNS = 4
 
@@ -20,6 +21,7 @@
 F32 = jnp.float32
 BF16 = jnp.bfloat16
 MASKED = -1e30
+VMEM_GRANT = 64 * 1024 * 1024
 
 VM = pl.BlockSpec(memory_space=pltpu.VMEM)
 SM = pl.BlockSpec(memory_space=pltpu.SMEM)
@@ -221,11 +223,13 @@
 
 
 def shifted_kernel(
-    seg_ref, place_ref, query_ref, pairs_ref,
+    seg_ref, place_ref, query_ref, zero_ref, one_ref, two_ref, three_ref,
     old_peak_ref, old_total_ref, old_acc_ref,
-    peak_ref, total_ref, acc_ref, heads_ref, score_ref,
+    peak_ref, total_ref, acc_ref, pairs_ref, heads_ref, score_ref,
 ):
     place = place_ref[0]
+    for column, column_ref in enumerate((zero_ref, one_ref, two_ref, three_ref)):
+        pairs_ref[column * ROWS : (column + 1) * ROWS] = column_ref[...]
     later_columns(
         pairs_ref, (1, COLUMNS), place % 2, seg_ref, place, query_ref,
         (old_peak_ref, old_total_ref, old_acc_ref), (peak_ref, total_ref, acc_ref),
@@ -256,28 +260,28 @@
 
 def local_memory(key, value, log_decay):
     return pl.pallas_call(
-        memory_kernel, name="memory", out_shape=shape(SEGS, 16, HEAD_DIM, dtype=BF16),
+        memory_kernel, name="memory", compiler_params=pltpu.CompilerParams(vmem_limit_bytes=VMEM_GRANT), out_shape=shape(SEGS, 16, HEAD_DIM, dtype=BF16),
         in_specs=[VM] * 3, out_specs=VM,
     )(key, value, log_decay)
 
 
 def scan_memory(received):
     return pl.pallas_call(
-        scan_kernel, name="scan", out_shape=shape(SEGS, 8, HEAD_DIM, dtype=BF16),
+        scan_kernel, name="scan", compiler_params=pltpu.CompilerParams(vmem_limit_bytes=VMEM_GRANT), out_shape=shape(SEGS, 8, HEAD_DIM, dtype=BF16),
         in_specs=[VM], out_specs=VM, scratch_shapes=[pltpu.VMEM((SEGS, 16, HEAD_DIM), F32)],
     )(received)
 
 
 def inside_part(query, key, value, log_decay):
     return pl.pallas_call(
-        inside_kernel, name="inside", out_shape=shape(TOK, HEADS_DEV * HEAD_DIM),
+        inside_kernel, name="inside", compiler_params=pltpu.CompilerParams(vmem_limit_bytes=VMEM_GRANT), out_shape=shape(TOK, HEADS_DEV * HEAD_DIM),
         in_specs=[VM] * 4, out_specs=VM,
     )(query, key, value, log_decay)
 
 
 def mixed_part(query, log_decay, inside, memory, shards):
     return pl.pallas_call(
-        mixed_kernel, name="mixed",
+        mixed_kernel, name="mixed", compiler_params=pltpu.CompilerParams(vmem_limit_bytes=VMEM_GRANT),
         out_shape=(shape(TOK, HEADS_DEV * HEAD_DIM), shape(shards, 8, TOK)),
         in_specs=[VM] * 4, out_specs=(VM, VM),
     )(query, log_decay, inside, memory)
@@ -285,14 +289,14 @@
 
 def gate_part(mixed, squares, gain, gate):
     return pl.pallas_call(
-        gate_kernel, name="gate", out_shape=shape(TOK, HEADS_DEV * HEAD_DIM, dtype=BF16),
+        gate_kernel, name="gate", compiler_params=pltpu.CompilerParams(vmem_limit_bytes=VMEM_GRANT), out_shape=shape(TOK, HEADS_DEV * HEAD_DIM, dtype=BF16),
         in_specs=[VM] * 4, out_specs=VM,
     )(mixed, squares, gain[None, :], gate)
 
 
 def key_value_pieces(place, key, value):
     return pl.pallas_call(
-        pieces_kernel, name="pieces",
+        pieces_kernel, name="pieces", compiler_params=pltpu.CompilerParams(vmem_limit_bytes=VMEM_GRANT),
         out_shape=shape(ROWS, TOK, 2 * HEAD_DIM, dtype=BF16),
         grid_spec=pltpu.PrefetchScalarGridSpec(
             num_scalar_prefetch=1,
@@ -323,7 +327,7 @@
 def attend_own(segment_of, place, query, pieces, column):
     whole = lambda *dims: pl.BlockSpec(dims, lambda i: (0,) * len(dims))
     return pl.pallas_call(
-        own_kernel, name="own",
+        own_kernel, name="own", compiler_params=pltpu.CompilerParams(vmem_limit_bytes=VMEM_GRANT),
         out_shape=(shape(STACKED, HEAD_DIM),) * 3,
         grid=(1,),
         in_specs=[
@@ -335,18 +339,18 @@
     )(segment_of, place, query, pieces, column)
 
 
-def attend_shifted(segment_of, place, query, pairs, state):
-    return pl.pallas_call(
-        shifted_kernel, name="shifted",
-        out_shape=(shape(STACKED, HEAD_DIM),) * 3,
-        in_specs=[SM, SM] + [VM] * 5, out_specs=(VM,) * 3,
+def attend_shifted(segment_of, place, query, columns, state):
+    return pl.pallas_call(
+        shifted_kernel, name="shifted", compiler_params=pltpu.CompilerParams(vmem_limit_bytes=VMEM_GRANT),
+        out_shape=(shape(STACKED, HEAD_DIM),) * 3 + (shape(HALF, TOK, 2 * HEAD_DIM, dtype=BF16),),
+        in_specs=[SM, SM] + [VM] * 8, out_specs=(VM,) * 4,
         scratch_shapes=score_scratch(COLUMNS - 1),
-    )(segment_of, place, query, pairs, *state)
+    )(segment_of, place, query, *columns, *state)
 
 
 def attend_swapped(segment_of, place, query, pairs, state):
     return pl.pallas_call(
-        swapped_kernel, name="swapped",
+        swapped_kernel, name="swapped", compiler_params=pltpu.CompilerParams(vmem_limit_bytes=VMEM_GRANT),
         out_shape=shape(TOK, HEADS_DEV * HEAD_DIM, dtype=BF16),
         in_specs=[SM, SM] + [VM] * 5, out_specs=VM,
         scratch_shapes=state_scratch(3) + score_scratch(COLUMNS),
@@ -377,8 +381,9 @@
     column = lax.all_to_all(
         pieces, "seq", 0, 0, tiled=True, axis_index_groups=same_column
     )
-    columns = [column] + [lax.ppermute(column, "seq", shifts[step]) for step in range(1, COLUMNS)]
-    pairs = jnp.concatenate(columns, axis=0)
+    columns = [column] + [
+        lax.ppermute(column, "seq", shifts[step]) for step in range(1, COLUMNS)
+    ]
     local = local_memory(lin_key, lin_value, log_decay)
     received = lax.all_to_all(local, "seq", 0, 0, tiled=True)
     scanned = scan_memory(received)
@@ -387,9 +392,9 @@
     mixed, squares = mixed_part(lin_query, log_decay, inside, memory, head_shards)
     squares = lax.all_to_all(squares, "head", 0, 0, tiled=True)
     lin_out = gate_part(mixed, squares, norm_gain, out_gate)
+    state = attend_own(segment_of, place, soft_query, pieces, column)
+    *state, pairs = attend_shifted(segment_of, place, soft_query, columns, state)
     others = lax.ppermute(pairs, "seq", partners)
-    state = attend_own(segment_of, place, soft_query, pieces, column)
-    state = attend_shifted(segment_of, place, soft_query, pairs, state)
     soft_out = attend_swapped(segment_of, place, soft_query, others, state)
     return (lin_out, soft_out)
 

time: 144 us -> 141 us (0.979)
  blocking collectives: 39.2 us -> 63.9 us
  starting transfers between devices: 37.6 us -> 23.5 us
  waiting for transfers between devices: 36.9 us -> 24.2 us
    all_to_all x0 -> x1, blocking collectives: none -> 24.7 us  [shards(): squares = lax.all_to_all(squares, 'head', 0, 0, tiled=True)]
    all_to_all x1 -> x0, starting transfers between devices: 14.9 us -> none  [shards(): squares = lax.all_to_all(squares, 'head', 0, 0, tiled=True)]
    all_to_all x1 -> x0, waiting for transfers between devices: 9.68 us -> none  [shards(): squares = lax.all_to_all(squares, 'head', 0, 0, tiled=True)]
    ppermute x3, waiting for transfers between devices: 18.7 us -> 15.5 us  [shards(): lax.ppermute(column, 'seq', shifts[step])]
  transfers between devices with their start and end apart: 6 -> 5, of which waited for: 5 -> 3; matrix products, arithmetic and copies ran while one was open for 0% -> 0% of each run, Pallas kernels for 14% -> 10%
where the time goes in v3:
time: 141 us; the launch traced here: 140 us
  blocking collectives  63.9 us (45%)
  Pallas kernels  28.1 us (20%)
  waiting for transfers between devices  24.2 us (17%)
  starting transfers between devices  23.5 us (17%)
    all_to_all x1, blocking collectives, shards(): squares = lax.all_to_all(squares, 'head', 0, 0, tiled=True)  24.7 us
    all_to_all x1, blocking collectives, shards(): lax.all_to_all(pieces, 'seq', 0, 0, tiled=True, axis_index_groups=same_co...  19.9 us
    all_to_all x1, blocking collectives, shards(): received = lax.all_to_all(local, 'seq', 0, 0, tiled=True)  19.4 us
    ppermute x3, waiting for transfers between devices, shards(): lax.ppermute(column, 'seq', shifts[step])  15.5 us
    ppermute x3, starting transfers between devices, shards(): lax.ppermute(column, 'seq', shifts[step])  14.5 us
    all_to_all x1, waiting for transfers between devices, shards(): memory = lax.all_to_all(scanned, 'seq', 0, 0, tiled=True)  8.74 us
    pallas_call x1, Pallas kernels, attend_swapped(): pl.pallas_call(swapped_kernel, name='swapped', compiler_params=pltpu.Comp...  6.52 us
    pallas_call x1, Pallas kernels, attend_shifted(): pl.pallas_call(shifted_kernel, name='shifted', compiler_params=pltpu.Comp...  6.07 us
  transfers between devices with their start and end apart: 5, of which 3 were waited for; matrix products, arithmetic and copies ran while one was open for 0% of the time, Pallas kernels for 10%

profile of v3, /device:TPU:1, one launch (start us, length us, event | category | flops | bytes accessed | tf_op | source)
XLA Modules:
  0.0 140.4 jit_solution(3325841789140618926)
XLA Ops:
  0.7 1.6 %pieces.1.own_ref = bf16[8,128,256]{2,1,0:T(8,128)(2,1)} custom-call(s32[1]{0:T(128)} %bitcast.2.place_ref, bf16[128,768]{1,0:T(8,128)(2,1)} %key_ref.5, bf16[128,768]{1,0:T(8,128)(2,1)} %value_ref.5), custom_call_target="tpu_custom_call" | custom-call | tf_op jit(solution)/shard_map/pieces/pallas_call | solution.py:298
  2.3 19.9 %all_to_all.20.column_ref.zero_ref = bf16[8,128,256]{2,1,0:T(8,128)(2,1)} all-to-all(bf16[8,128,256]{2,1,0:T(8,128)(2,1)} %pieces.1.own_ref), channel_id=1, replica_groups={{0,96,192,288,384,480,576,672},{12,108,204,300,396,492,588,684},{24,120..., dimensions={0} | all-to-all | bytes 1048576 | tf_op jit(solution)/shard_map/all_to_all | solution.py:381
  22.2 7.1 %collective-permute-start = (bf16[8,128,256]{2,1,0:T(8,128)(2,1)}, bf16[8,128,256]{2,1,0:T(8,128)(2,1)}, u32[]{:S(2)}, u32[]{:S(2)}) collective-permute-start(bf16[8,128,256]{2,1,0:T(8,128)(2,1)} %all_to_all.20.column_ref.zero_ref), channel_id=1, source_target_pairs={{0,24},{12,36},{24,48},{36,60},{48,72},{60,84},{72,0},{84,12},{96,... | collective-permute-start | bytes 1572872 | tf_op jit(solution)/shard_map/ppermute | solution.py:385
  29.3 4.4 %collective-permute-start.1 = (bf16[8,128,256]{2,1,0:T(8,128)(2,1)}, bf16[8,128,256]{2,1,0:T(8,128)(2,1)}, u32[]{:S(2)}, u32[]{:S(2)}) collective-permute-start(bf16[8,128,256]{2,1,0:T(8,128)(2,1)} %all_to_all.20.column_ref.zero_ref), channel_id=1, source_target_pairs={{0,48},{12,60},{24,72},{36,84},{48,0},{60,12},{72,24},{84,36},{96,... | collective-permute-start | bytes 1572872 | tf_op jit(solution)/shard_map/ppermute | solution.py:385
  33.6 3.1 %collective-permute-start.2 = (bf16[8,128,256]{2,1,0:T(8,128)(2,1)}, bf16[8,128,256]{2,1,0:T(8,128)(2,1)}, u32[]{:S(2)}, u32[]{:S(2)}) collective-permute-start(bf16[8,128,256]{2,1,0:T(8,128)(2,1)} %all_to_all.20.column_ref.zero_ref), channel_id=1, source_target_pairs={{0,72},{12,84},{24,0},{36,12},{48,24},{60,36},{72,48},{84,60},{96,... | collective-permute-start | bytes 1572872 | tf_op jit(solution)/shard_map/ppermute | solution.py:385
  36.7 3.3 %own.1 = (f32[512,128]{1,0:T(8,128)}, f32[512,128]{1,0:T(8,128)}, f32[512,128]{1,0:T(8,128)}) custom-call(s32[64]{0:T(128)} %seg_ref.5, s32[1]{0:T(128)} %bitcast.1.place_ref, bf16[128,512]{1,0:T(8,128)(2,1)} %query_ref.9, bf16[8,128,256]{2,1,0:T(8,128)(2,1)} %pieces.1.own_ref, bf16[8,128,256]{2,1,0:T(8,128)(2,1)} %all_to_all.20.column_ref.zero_ref), custom_call_target="tpu_custom_call" | custom-call | tf_op jit(solution)/shard_map/own/pallas_call | solution.py:329
  40.0 0.0 collective-permute-done.one_ref
  40.0 12.9 %collective-permute-done.1.two_ref = bf16[8,128,256]{2,1,0:T(8,128)(2,1)} collective-permute-done((bf16[8,128,256]{2,1,0:T(8,128)(2,1)}, bf16[8,128,256]{2,1,0:T(8,128)(2,1)}, u32[]{:S(2)}, u32[]{:S(2)}) %collective-permute-start.1) | collective-permute-done | bytes 524320 | tf_op jit(solution)/shard_map/ppermute | solution.py:385
  52.9 2.6 %collective-permute-done.2.three_ref = bf16[8,128,256]{2,1,0:T(8,128)(2,1)} collective-permute-done((bf16[8,128,256]{2,1,0:T(8,128)(2,1)}, bf16[8,128,256]{2,1,0:T(8,128)(2,1)}, u32[]{:S(2)}, u32[]{:S(2)}) %collective-permute-start.2) | collective-permute-done | bytes 524320 | tf_op jit(solution)/shard_map/ppermute | solution.py:385
  55.5 6.1 %shifted.1 = (f32[512,128]{1,0:T(8,128)}, f32[512,128]{1,0:T(8,128)}, f32[512,128]{1,0:T(8,128)}, bf16[32,128,256]{2,1,0:T(8,128)(2,1)}) custom-call(s32[64]{0:T(128)} %seg_ref.5, s32[1]{0:T(128)} %bitcast.1.place_ref, bf16[128,512]{1,0:T(8,128)(2,1)} %query_ref.9, bf16[8,128,256]{2,1,0:T(8,128)(2,1)} %all_to_all.20.column_ref.zero_ref, ...), custom_call_target="tpu_custom_call" | custom-call | tf_op jit(solution)/shard_map/shifted/pallas_call | solution.py:343
  61.6 3.9 %collective-permute-start.3 = (bf16[32,128,256]{2,1,0:T(8,128)(2,1)}, bf16[32,128,256]{2,1,0:T(8,128)(2,1)}, u32[]{:S(2)}, u32[]{:S(2)}) collective-permute-start(bf16[32,128,256]{2,1,0:T(8,128)(2,1)} %get-tuple-element.16), channel_id=1, source_target_pairs={{0,12},{12,0},{24,36},{36,24},{48,60},{60,48},{72,84},{84,72},{96,... | collective-permute-start | bytes 6291464 | tf_op jit(solution)/shard_map/ppermute | solution.py:397
  65.5 2.0 %memory.1 = bf16[64,16,128]{2,1,0:T(8,128)(2,1)} custom-call(bf16[128,512]{1,0:T(8,128)(2,1)} %key_ref.4, bf16[128,512]{1,0:T(8,128)(2,1)} %value_ref.4, f32[4,128]{1,0:T(4,128)} %log_ref.5), custom_call_target="tpu_custom_call" | custom-call | tf_op jit(solution)/shard_map/memory/pallas_call | solution.py:262
  67.5 19.4 %all_to_all.21.in_ref = bf16[64,16,128]{2,1,0:T(8,128)(2,1)} all-to-all(bf16[64,16,128]{2,1,0:T(8,128)(2,1)} %memory.1), channel_id=1, replica_groups=mesh['seq'=64,'head'=12] {'seq'}, dimensions={0} | all-to-all | bytes 524288 | tf_op jit(solution)/shard_map/all_to_all | solution.py:388
  86.9 2.3 %scan.1 = bf16[64,8,128]{2,1,0:T(8,128)(2,1)} custom-call(bf16[64,16,128]{2,1,0:T(8,128)(2,1)} %all_to_all.21.in_ref), custom_call_target="tpu_custom_call" | custom-call | tf_op jit(solution)/shard_map/scan/pallas_call | solution.py:269
  89.1 5.1 %all-to-all-start.1 = ((bf16[64,8,128]{2,1,0:T(8,128)(2,1)}), bf16[64,8,128]{2,1,0:T(8,128)(2,1)}, u32[]{:S(2)}, u32[]{:S(2)}) async-start(bf16[64,8,128]{2,1,0:T(8,128)(2,1)} %scan.1), calls=%async_computation.1 | async-start | bytes 262144 | tf_op jit(solution)/shard_map/all_to_all | solution.py:390
  94.2 2.5 %inside.1.inside_ref = f32[128,512]{1,0:T(8,128)} custom-call(bf16[128,512]{1,0:T(8,128)(2,1)} %query_ref.6, bf16[128,512]{1,0:T(8,128)(2,1)} %key_ref.4, bf16[128,512]{1,0:T(8,128)(2,1)} %value_ref.4, f32[4,128]{1,0:T(4,128)} %log_ref.5), custom_call_target="tpu_custom_call" | custom-call | tf_op jit(solution)/shard_map/inside/pallas_call | solution.py:276
  96.7 8.7 %all-to-all-done.1.memory_ref = bf16[64,8,128]{2,1,0:T(8,128)(2,1)} async-done(((bf16[64,8,128]{2,1,0:T(8,128)(2,1)}), bf16[64,8,128]{2,1,0:T(8,128)(2,1)}, u32[]{:S(2)}, u32[]{:S(2)}) %all-to-all-start.1) | async-done | bytes 131104 | tf_op jit(solution)/shard_map/all_to_all | solution.py:390
  105.5 2.0 %mixed.1 = (f32[128,512]{1,0:T(8,128)}, f32[12,8,128]{2,1,0:T(8,128)}) custom-call(bf16[128,512]{1,0:T(8,128)(2,1)} %query_ref.6, f32[4,128]{1,0:T(4,128)} %log_ref.5, f32[128,512]{1,0:T(8,128)} %inside.1.inside_ref, bf16[64,8,128]{2,1,0:T(8,128)(2,1)} %all-to-all-done.1.memory_ref), custom_call_target="tpu_custom_call" | custom-call | tf_op jit(solution)/shard_map/mixed/pallas_call | solution.py:283
  107.4 24.7 %all_to_all.22.square_ref = f32[12,8,128]{2,1,0:T(8,128)} all-to-all(f32[12,8,128]{2,1,0:T(8,128)} %get-tuple-element.12), channel_id=1, replica_groups=mesh['seq'=64,'head'=12] {'head'}, dimensions={0} | all-to-all | bytes 98304 | tf_op jit(solution)/shard_map/all_to_all | solution.py:393
  132.1 1.8 %gate.1 = bf16[128,512]{1,0:T(8,128)(2,1)} custom-call(f32[128,512]{1,0:T(8,128)} %get-tuple-element.11.mixed_ref, f32[12,8,128]{2,1,0:T(8,128)} %all_to_all.22.square_ref, f32[1,512]{1,0:T(1,128)} %bitcast.3, bf16[128,512]{1,0:T(8,128)(2,1)} %gate_ref.1), custom_call_target="tpu_custom_call" | custom-call | tf_op jit(solution)/shard_map/gate/pallas_call | solution.py:291
  133.9 0.0 collective-permute-done.3.pairs_ref
  133.9 6.5 %swapped.1 = bf16[128,512]{1,0:T(8,128)(2,1)} custom-call(s32[64]{0:T(128)} %seg_ref.5, s32[1]{0:T(128)} %bitcast.1.place_ref, bf16[128,512]{1,0:T(8,128)(2,1)} %query_ref.9, bf16[32,128,256]{2,1,0:T(8,128)(2,1)} %collective-permute-done.3.pairs_ref, f32[512,128]{1,0:T(8,128)} %get-tuple-element.17.old_peak_ref, f32[512,128]{1,0:T(8,128)} %get-tuple-element.18.old_total_ref, ...), custom_call_target="tpu_custom_call" | custom-call | tf_op jit(solution)/shard_map/swapped/pallas_call | solution.py:352
Async XLA Ops:
  22.2 17.8 %collective-permute-start = (bf16[8,128,256]{2,1,0:T(8,128)(2,1)}, bf16[8,128,256]{2,1,0:T(8,128)(2,1)}, u32[]{:S(2)}, u32[]{:S(2)}) collective-permute-start(bf16[8,128,256]{2,1,0:T(8,128)(2,1)} %all_to_all.20.column_ref.zero_ref), channel_id=1, source_target_pairs={{0,24},{12,36},{24,48},{36,60},{48,72},{60,84},{72,0},{84,12},{96,... | collective-permute-start | bytes 1572872 | tf_op jit(solution)/shard_map/ppermute | solution.py:385
  29.3 23.7 %collective-permute-start.1 = (bf16[8,128,256]{2,1,0:T(8,128)(2,1)}, bf16[8,128,256]{2,1,0:T(8,128)(2,1)}, u32[]{:S(2)}, u32[]{:S(2)}) collective-permute-start(bf16[8,128,256]{2,1,0:T(8,128)(2,1)} %all_to_all.20.column_ref.zero_ref), channel_id=1, source_target_pairs={{0,48},{12,60},{24,72},{36,84},{48,0},{60,12},{72,24},{84,36},{96,... | collective-permute-start | bytes 1572872 | tf_op jit(solution)/shard_map/ppermute | solution.py:385
  33.6 21.9 %collective-permute-start.2 = (bf16[8,128,256]{2,1,0:T(8,128)(2,1)}, bf16[8,128,256]{2,1,0:T(8,128)(2,1)}, u32[]{:S(2)}, u32[]{:S(2)}) collective-permute-start(bf16[8,128,256]{2,1,0:T(8,128)(2,1)} %all_to_all.20.column_ref.zero_ref), channel_id=1, source_target_pairs={{0,72},{12,84},{24,0},{36,12},{48,24},{60,36},{72,48},{84,60},{96,... | collective-permute-start | bytes 1572872 | tf_op jit(solution)/shard_map/ppermute | solution.py:385
  61.6 72.3 %collective-permute-start.3 = (bf16[32,128,256]{2,1,0:T(8,128)(2,1)}, bf16[32,128,256]{2,1,0:T(8,128)(2,1)}, u32[]{:S(2)}, u32[]{:S(2)}) collective-permute-start(bf16[32,128,256]{2,1,0:T(8,128)(2,1)} %get-tuple-element.16), channel_id=1, source_target_pairs={{0,12},{12,0},{24,36},{36,24},{48,60},{60,48},{72,84},{84,72},{96,... | collective-permute-start | bytes 6291464 | tf_op jit(solution)/shard_map/ppermute | solution.py:397
  89.1 16.4 %all-to-all-start.1 = ((bf16[64,8,128]{2,1,0:T(8,128)(2,1)}), bf16[64,8,128]{2,1,0:T(8,128)(2,1)}, u32[]{:S(2)}, u32[]{:S(2)}) async-start(bf16[64,8,128]{2,1,0:T(8,128)(2,1)} %scan.1), calls=%async_computation.1 | async-start | bytes 262144 | tf_op jit(solution)/shard_map/all_to_all | solution.py:390

commit v4 on v3

--- a/solution.py
+++ b/solution.py
@@ -151,7 +151,7 @@
     own_segment = seg_ref[place]
 
     def score(column, carry):
-        source = jnp.bitwise_and(place // 2 - column, COLUMNS - 1)
+        source = jnp.bitwise_and(place // 2 - column * (1 - 2 * core), COLUMNS - 1)
         keys = pairs_ref[pl.ds(column * ROWS, ROWS), :, 0:HEAD_DIM].reshape(ROWS * TOK, HEAD_DIM)
         logits = dot(heads_ref[...], keys, 1, 1)
         top = top_ref[...]
@@ -163,7 +163,7 @@
         top_ref[...] = top
         return carry
 
-    lax.fori_loop(*columns, score, 0)
+    lax.fori_loop(*columns, score, 0, unroll=2)
 
 
 def weigh_columns(pairs_ref, columns, score_ref, peak_ref, total_ref, acc_ref):
@@ -370,20 +370,20 @@
     segment_of,
 ):
     place = lax.axis_index("seq").astype(jnp.int32)[None]
-    shared = (lax.axis_index("head") * HEADS_DEV // Q_PER_KV).astype(jnp.int32)[None]
+    shared = lax.div(lax.axis_index("head").astype(jnp.int32), Q_PER_KV // HEADS_DEV)[None]
     head_shards = lax.axis_size("head")
     same_column = [[row * 8 + at for row in range(ROWS)] for at in range(8)]
-    shifts = [
-        [(at, at // 8 * 8 + (at + 2 * step) % 8) for at in range(SEGS)] for step in range(COLUMNS)
-    ]
+    ahead = [(at, at // 8 * 8 + (at + 2 * (1 - 2 * (at % 2))) % 8) for at in range(SEGS)]
+    back = [(there, here) for here, there in ahead]
     partners = [(at, at ^ 1) for at in range(SEGS)]
     pieces = key_value_pieces(shared, soft_key, soft_value)
     column = lax.all_to_all(
         pieces, "seq", 0, 0, tiled=True, axis_index_groups=same_column
     )
-    columns = [column] + [
-        lax.ppermute(column, "seq", shifts[step]) for step in range(1, COLUMNS)
-    ]
+    nearest = lax.ppermute(column, "seq", ahead)
+    behind = lax.ppermute(column, "seq", back)
+    farthest = lax.ppermute(nearest, "seq", ahead)
+    columns = [column, nearest, farthest, behind]
     local = local_memory(lin_key, lin_value, log_decay)
     received = lax.all_to_all(local, "seq", 0, 0, tiled=True)
     scanned = scan_memory(received)

time: 141 us -> 139 us (0.986)
  starting transfers between devices: 23.5 us -> 33.7 us
  waiting for transfers between devices: 24.2 us -> 17.4 us
  blocking collectives: 63.9 us -> 59.3 us
    ppermute x1, starting transfers between devices: 3.89 us -> 13.3 us  [shards(): others = lax.ppermute(pairs, 'seq', partners)]
    ppermute x3, waiting for transfers between devices: 15.5 us -> 8.69 us  [the longest x1 4.49 us: shards(): nearest = lax.ppermute(column, 'seq', ahead)]
    all_to_all x1, blocking collectives: 24.7 us -> 21.5 us  [shards(): squares = lax.all_to_all(squares, 'head', 0, 0, tiled=True)]
  transfers between devices with their start and end apart: 5 -> 5, of which waited for: 3 -> 4; matrix products, arithmetic and copies ran while one was open for 0% -> 0% of each run, Pallas kernels for 10% -> 10%
where the time goes in v4:
time: 139 us; the launch traced here: 138 us
  blocking collectives  59.3 us (43%)
  starting transfers between devices  33.7 us (24%)
  Pallas kernels  27.3 us (20%)
  waiting for transfers between devices  17.4 us (13%)
    all_to_all x1, blocking collectives, shards(): squares = lax.all_to_all(squares, 'head', 0, 0, tiled=True)  21.5 us
    all_to_all x1, blocking collectives, shards(): lax.all_to_all(pieces, 'seq', 0, 0, tiled=True, axis_index_groups=same_co...  19.9 us
    all_to_all x1, blocking collectives, shards(): received = lax.all_to_all(local, 'seq', 0, 0, tiled=True)  18 us
    ppermute x1, starting transfers between devices, shards(): others = lax.ppermute(pairs, 'seq', partners)  13.3 us
    all_to_all x1, waiting for transfers between devices, shards(): memory = lax.all_to_all(scanned, 'seq', 0, 0, tiled=True)  8.74 us
    ppermute x1, starting transfers between devices, shards(): nearest = lax.ppermute(column, 'seq', ahead)  8.34 us
    pallas_call x1, Pallas kernels, attend_swapped(): pl.pallas_call(swapped_kernel, name='swapped', compiler_params=pltpu.Comp...  6.18 us
    pallas_call x1, Pallas kernels, attend_shifted(): pl.pallas_call(shifted_kernel, name='shifted', compiler_params=pltpu.Comp...  5.59 us
  transfers between devices with their start and end apart: 5, of which 4 were waited for; matrix products, arithmetic and copies ran while one was open for 0% of the time, Pallas kernels for 10%

profile of v4, /device:TPU:1, one launch (start us, length us, event | category | flops | bytes accessed | tf_op | source)
XLA Modules:
  0.0 138.4 jit_solution(17886731883598946470)
XLA Ops:
  0.6 1.6 %pieces.1.own_ref = bf16[8,128,256]{2,1,0:T(8,128)(2,1)} custom-call(s32[1]{0:T(128)} %bitcast.2.place_ref, bf16[128,768]{1,0:T(8,128)(2,1)} %key_ref.5, bf16[128,768]{1,0:T(8,128)(2,1)} %value_ref.5), custom_call_target="tpu_custom_call" | custom-call | tf_op jit(solution)/shard_map/pieces/pallas_call | solution.py:298
  2.3 19.9 %all_to_all.20.column_ref.zero_ref = bf16[8,128,256]{2,1,0:T(8,128)(2,1)} all-to-all(bf16[8,128,256]{2,1,0:T(8,128)(2,1)} %pieces.1.own_ref), channel_id=1, replica_groups={{0,96,192,288,384,480,576,672},{12,108,204,300,396,492,588,684},{24,120..., dimensions={0} | all-to-all | bytes 1048576 | tf_op jit(solution)/shard_map/all_to_all | solution.py:380
  22.2 8.3 %collective-permute-start = (bf16[8,128,256]{2,1,0:T(8,128)(2,1)}, bf16[8,128,256]{2,1,0:T(8,128)(2,1)}, u32[]{:S(2)}, u32[]{:S(2)}) collective-permute-start(bf16[8,128,256]{2,1,0:T(8,128)(2,1)} %all_to_all.20.column_ref.zero_ref), channel_id=1, source_target_pairs={{0,24},{12,84},{24,48},{36,12},{48,72},{60,36},{72,0},{84,60},{96,... | collective-permute-start | bytes 1572872 | tf_op jit(solution)/shard_map/ppermute | solution.py:383
  30.5 1.9 %collective-permute-start.2 = (bf16[8,128,256]{2,1,0:T(8,128)(2,1)}, bf16[8,128,256]{2,1,0:T(8,128)(2,1)}, u32[]{:S(2)}, u32[]{:S(2)}) collective-permute-start(bf16[8,128,256]{2,1,0:T(8,128)(2,1)} %all_to_all.20.column_ref.zero_ref), channel_id=1, source_target_pairs={{24,0},{84,12},{48,24},{12,36},{72,48},{36,60},{0,72},{60,84},{120... | collective-permute-start | bytes 1572872 | tf_op jit(solution)/shard_map/ppermute | solution.py:384
  32.5 4.5 %collective-permute-done.one_ref = bf16[8,128,256]{2,1,0:T(8,128)(2,1)} collective-permute-done((bf16[8,128,256]{2,1,0:T(8,128)(2,1)}, bf16[8,128,256]{2,1,0:T(8,128)(2,1)}, u32[]{:S(2)}, u32[]{:S(2)}) %collective-permute-start) | collective-permute-done | bytes 524320 | tf_op jit(solution)/shard_map/ppermute | solution.py:383
  37.0 5.0 %collective-permute-start.1 = (bf16[8,128,256]{2,1,0:T(8,128)(2,1)}, bf16[8,128,256]{2,1,0:T(8,128)(2,1)}, u32[]{:S(2)}, u32[]{:S(2)}) collective-permute-start(bf16[8,128,256]{2,1,0:T(8,128)(2,1)} %collective-permute-done.one_ref), channel_id=1, source_target_pairs={{0,24},{12,84},{24,48},{36,12},{48,72},{60,36},{72,0},{84,60},{96,... | collective-permute-start | bytes 1572872 | tf_op jit(solution)/shard_map/ppermute | solution.py:385
  42.0 3.3 %own.1 = (f32[512,128]{1,0:T(8,128)}, f32[512,128]{1,0:T(8,128)}, f32[512,128]{1,0:T(8,128)}) custom-call(s32[64]{0:T(128)} %seg_ref.5, s32[1]{0:T(128)} %bitcast.1.place_ref, bf16[128,512]{1,0:T(8,128)(2,1)} %query_ref.9, bf16[8,128,256]{2,1,0:T(8,128)(2,1)} %pieces.1.own_ref, bf16[8,128,256]{2,1,0:T(8,128)(2,1)} %all_to_all.20.column_ref.zero_ref), custom_call_target="tpu_custom_call" | custom-call | tf_op jit(solution)/shard_map/own/pallas_call | solution.py:329
  45.3 2.5 %collective-permute-done.2.three_ref = bf16[8,128,256]{2,1,0:T(8,128)(2,1)} collective-permute-done((bf16[8,128,256]{2,1,0:T(8,128)(2,1)}, bf16[8,128,256]{2,1,0:T(8,128)(2,1)}, u32[]{:S(2)}, u32[]{:S(2)}) %collective-permute-start.2) | collective-permute-done | bytes 524320 | tf_op jit(solution)/shard_map/ppermute | solution.py:384
  47.8 1.7 %collective-permute-done.1.two_ref = bf16[8,128,256]{2,1,0:T(8,128)(2,1)} collective-permute-done((bf16[8,128,256]{2,1,0:T(8,128)(2,1)}, bf16[8,128,256]{2,1,0:T(8,128)(2,1)}, u32[]{:S(2)}, u32[]{:S(2)}) %collective-permute-start.1) | collective-permute-done | bytes 524320 | tf_op jit(solution)/shard_map/ppermute | solution.py:385
  49.5 5.6 %shifted.1 = (f32[512,128]{1,0:T(8,128)}, f32[512,128]{1,0:T(8,128)}, f32[512,128]{1,0:T(8,128)}, bf16[32,128,256]{2,1,0:T(8,128)(2,1)}) custom-call(s32[64]{0:T(128)} %seg_ref.5, s32[1]{0:T(128)} %bitcast.1.place_ref, bf16[128,512]{1,0:T(8,128)(2,1)} %query_ref.9, bf16[8,128,256]{2,1,0:T(8,128)(2,1)} %all_to_all.20.column_ref.zero_ref, ...), custom_call_target="tpu_custom_call" | custom-call | tf_op jit(solution)/shard_map/shifted/pallas_call | solution.py:343
  55.1 13.3 %collective-permute-start.3 = (bf16[32,128,256]{2,1,0:T(8,128)(2,1)}, bf16[32,128,256]{2,1,0:T(8,128)(2,1)}, u32[]{:S(2)}, u32[]{:S(2)}) collective-permute-start(bf16[32,128,256]{2,1,0:T(8,128)(2,1)} %get-tuple-element.16), channel_id=1, source_target_pairs={{0,12},{12,0},{24,36},{36,24},{48,60},{60,48},{72,84},{84,72},{96,... | collective-permute-start | bytes 6291464 | tf_op jit(solution)/shard_map/ppermute | solution.py:397
  68.4 2.0 %memory.1 = bf16[64,16,128]{2,1,0:T(8,128)(2,1)} custom-call(bf16[128,512]{1,0:T(8,128)(2,1)} %key_ref.4, bf16[128,512]{1,0:T(8,128)(2,1)} %value_ref.4, f32[4,128]{1,0:T(4,128)} %log_ref.5), custom_call_target="tpu_custom_call" | custom-call | tf_op jit(solution)/shard_map/memory/pallas_call | solution.py:262
  70.4 18.0 %all_to_all.21.in_ref = bf16[64,16,128]{2,1,0:T(8,128)(2,1)} all-to-all(bf16[64,16,128]{2,1,0:T(8,128)(2,1)} %memory.1), channel_id=1, replica_groups=mesh['seq'=64,'head'=12] {'seq'}, dimensions={0} | all-to-all | bytes 524288 | tf_op jit(solution)/shard_map/all_to_all | solution.py:388
  88.4 2.3 %scan.1 = bf16[64,8,128]{2,1,0:T(8,128)(2,1)} custom-call(bf16[64,16,128]{2,1,0:T(8,128)(2,1)} %all_to_all.21.in_ref), custom_call_target="tpu_custom_call" | custom-call | tf_op jit(solution)/shard_map/scan/pallas_call | solution.py:269
  90.6 5.1 %all-to-all-start.1 = ((bf16[64,8,128]{2,1,0:T(8,128)(2,1)}), bf16[64,8,128]{2,1,0:T(8,128)(2,1)}, u32[]{:S(2)}, u32[]{:S(2)}) async-start(bf16[64,8,128]{2,1,0:T(8,128)(2,1)} %scan.1), calls=%async_computation.1 | async-start | bytes 262144 | tf_op jit(solution)/shard_map/all_to_all | solution.py:390
  95.8 2.5 %inside.1.inside_ref = f32[128,512]{1,0:T(8,128)} custom-call(bf16[128,512]{1,0:T(8,128)(2,1)} %query_ref.6, bf16[128,512]{1,0:T(8,128)(2,1)} %key_ref.4, bf16[128,512]{1,0:T(8,128)(2,1)} %value_ref.4, f32[4,128]{1,0:T(4,128)} %log_ref.5), custom_call_target="tpu_custom_call" | custom-call | tf_op jit(solution)/shard_map/inside/pallas_call | solution.py:276
  98.3 8.7 %all-to-all-done.1.memory_ref = bf16[64,8,128]{2,1,0:T(8,128)(2,1)} async-done(((bf16[64,8,128]{2,1,0:T(8,128)(2,1)}), bf16[64,8,128]{2,1,0:T(8,128)(2,1)}, u32[]{:S(2)}, u32[]{:S(2)}) %all-to-all-start.1) | async-done | bytes 131104 | tf_op jit(solution)/shard_map/all_to_all | solution.py:390
  107.0 2.0 %mixed.1 = (f32[128,512]{1,0:T(8,128)}, f32[12,8,128]{2,1,0:T(8,128)}) custom-call(bf16[128,512]{1,0:T(8,128)(2,1)} %query_ref.6, f32[4,128]{1,0:T(4,128)} %log_ref.5, f32[128,512]{1,0:T(8,128)} %inside.1.inside_ref, bf16[64,8,128]{2,1,0:T(8,128)(2,1)} %all-to-all-done.1.memory_ref), custom_call_target="tpu_custom_call" | custom-call | tf_op jit(solution)/shard_map/mixed/pallas_call | solution.py:283
  109.0 21.5 %all_to_all.22.square_ref = f32[12,8,128]{2,1,0:T(8,128)} all-to-all(f32[12,8,128]{2,1,0:T(8,128)} %get-tuple-element.12), channel_id=1, replica_groups=mesh['seq'=64,'head'=12] {'head'}, dimensions={0} | all-to-all | bytes 98304 | tf_op jit(solution)/shard_map/all_to_all | solution.py:393
  130.4 1.8 %gate.1 = bf16[128,512]{1,0:T(8,128)(2,1)} custom-call(f32[128,512]{1,0:T(8,128)} %get-tuple-element.11.mixed_ref, f32[12,8,128]{2,1,0:T(8,128)} %all_to_all.22.square_ref, f32[1,512]{1,0:T(1,128)} %bitcast.3, bf16[128,512]{1,0:T(8,128)(2,1)} %gate_ref.1), custom_call_target="tpu_custom_call" | custom-call | tf_op jit(solution)/shard_map/gate/pallas_call | solution.py:291
  132.2 0.0 collective-permute-done.3.pairs_ref
  132.2 6.2 %swapped.1 = bf16[128,512]{1,0:T(8,128)(2,1)} custom-call(s32[64]{0:T(128)} %seg_ref.5, s32[1]{0:T(128)} %bitcast.1.place_ref, bf16[128,512]{1,0:T(8,128)(2,1)} %query_ref.9, bf16[32,128,256]{2,1,0:T(8,128)(2,1)} %collective-permute-done.3.pairs_ref, f32[512,128]{1,0:T(8,128)} %get-tuple-element.17.old_peak_ref, f32[512,128]{1,0:T(8,128)} %get-tuple-element.18.old_total_ref, ...), custom_call_target="tpu_custom_call" | custom-call | tf_op jit(solution)/shard_map/swapped/pallas_call | solution.py:352
Async XLA Ops:
  22.2 14.8 %collective-permute-start = (bf16[8,128,256]{2,1,0:T(8,128)(2,1)}, bf16[8,128,256]{2,1,0:T(8,128)(2,1)}, u32[]{:S(2)}, u32[]{:S(2)}) collective-permute-start(bf16[8,128,256]{2,1,0:T(8,128)(2,1)} %all_to_all.20.column_ref.zero_ref), channel_id=1, source_target_pairs={{0,24},{12,84},{24,48},{36,12},{48,72},{60,36},{72,0},{84,60},{96,... | collective-permute-start | bytes 1572872 | tf_op jit(solution)/shard_map/ppermute | solution.py:383
  30.5 17.3 %collective-permute-start.2 = (bf16[8,128,256]{2,1,0:T(8,128)(2,1)}, bf16[8,128,256]{2,1,0:T(8,128)(2,1)}, u32[]{:S(2)}, u32[]{:S(2)}) collective-permute-start(bf16[8,128,256]{2,1,0:T(8,128)(2,1)} %all_to_all.20.column_ref.zero_ref), channel_id=1, source_target_pairs={{24,0},{84,12},{48,24},{12,36},{72,48},{36,60},{0,72},{60,84},{120... | collective-permute-start | bytes 1572872 | tf_op jit(solution)/shard_map/ppermute | solution.py:384
  37.0 12.5 %collective-permute-start.1 = (bf16[8,128,256]{2,1,0:T(8,128)(2,1)}, bf16[8,128,256]{2,1,0:T(8,128)(2,1)}, u32[]{:S(2)}, u32[]{:S(2)}) collective-permute-start(bf16[8,128,256]{2,1,0:T(8,128)(2,1)} %collective-permute-done.one_ref), channel_id=1, source_target_pairs={{0,24},{12,84},{24,48},{36,12},{48,72},{60,36},{72,0},{84,60},{96,... | collective-permute-start | bytes 1572872 | tf_op jit(solution)/shard_map/ppermute | solution.py:385
  55.1 77.2 %collective-permute-start.3 = (bf16[32,128,256]{2,1,0:T(8,128)(2,1)}, bf16[32,128,256]{2,1,0:T(8,128)(2,1)}, u32[]{:S(2)}, u32[]{:S(2)}) collective-permute-start(bf16[32,128,256]{2,1,0:T(8,128)(2,1)} %get-tuple-element.16), channel_id=1, source_target_pairs={{0,12},{12,0},{24,36},{36,24},{48,60},{60,48},{72,84},{84,72},{96,... | collective-permute-start | bytes 6291464 | tf_op jit(solution)/shard_map/ppermute | solution.py:397
  90.6 16.4 %all-to-all-start.1 = ((bf16[64,8,128]{2,1,0:T(8,128)(2,1)}), bf16[64,8,128]{2,1,0:T(8,128)(2,1)}, u32[]{:S(2)}, u32[]{:S(2)}) async-start(bf16[64,8,128]{2,1,0:T(8,128)(2,1)} %scan.1), calls=%async_computation.1 | async-start | bytes 262144 | tf_op jit(solution)/shard_map/all_to_all | solution.py:390

commit v5 on v4

--- a/solution.py
+++ b/solution.py
@@ -14,6 +14,7 @@
 HALF = 32
 ROWS = 8
 COLUMNS = 4
+TURN = 4
 
 norm_eps = 1e-06
 SCALE = HEAD_DIM ** (-0.5)
@@ -156,7 +157,8 @@
         logits = dot(heads_ref[...], keys, 1, 1)
         top = top_ref[...]
         for at in range(ROWS):
-            seg = seg_ref[at * ROWS + source * 2 + core]
+            row = jnp.bitwise_and(at + TURN * core, ROWS - 1)
+            seg = seg_ref[row * ROWS + source * 2 + core]
             part = logits[:, at * TOK : (at + 1) * TOK] + jnp.where(seg < own_segment, 0.0, MASKED).astype(F32)
             top = jnp.maximum(top, part)
             score_ref[column - columns[0], :, at * TOK : (at + 1) * TOK] = part
@@ -372,7 +374,9 @@
     place = lax.axis_index("seq").astype(jnp.int32)[None]
     shared = lax.div(lax.axis_index("head").astype(jnp.int32), Q_PER_KV // HEADS_DEV)[None]
     head_shards = lax.axis_size("head")
-    same_column = [[row * 8 + at for row in range(ROWS)] for at in range(8)]
+    same_column = [
+        [(rank + TURN * (at % 2)) % ROWS * 8 + at for rank in range(ROWS)] for at in range(8)
+    ]
     ahead = [(at, at // 8 * 8 + (at + 2 * (1 - 2 * (at % 2))) % 8) for at in range(SEGS)]
     back = [(there, here) for here, there in ahead]
     partners = [(at, at ^ 1) for at in range(SEGS)]

time: 139 us -> 139 us (level)
  blocking collectives: 59.3 us -> 56.9 us
  starting transfers between devices: 33.7 us -> 35.1 us
    all_to_all x1, blocking collectives: 19.9 us -> 17.5 us  [shards(): lax.all_to_all(pieces, 'seq', 0, 0, tiled=True, axis_index_groups=same_co...]
    ppermute x1, starting transfers between devices: 8.34 us -> 10.1 us  [shards(): nearest = lax.ppermute(column, 'seq', ahead)]
where the time goes in v5:
time: 139 us; the launch traced here: 138 us
  blocking collectives  56.9 us (41%)
  starting transfers between devices  35.1 us (25%)
  Pallas kernels  27.3 us (20%)
  waiting for transfers between devices  17.9 us (13%)
    all_to_all x1, blocking collectives, shards(): squares = lax.all_to_all(squares, 'head', 0, 0, tiled=True)  21.4 us
    all_to_all x1, blocking collectives, shards(): received = lax.all_to_all(local, 'seq', 0, 0, tiled=True)  18 us
    all_to_all x1, blocking collectives, shards(): lax.all_to_all(pieces, 'seq', 0, 0, tiled=True, axis_index_groups=same_co...  17.5 us
    ppermute x1, starting transfers between devices, shards(): others = lax.ppermute(pairs, 'seq', partners)  12.9 us
    ppermute x1, starting transfers between devices, shards(): nearest = lax.ppermute(column, 'seq', ahead)  10.1 us
    all_to_all x1, waiting for transfers between devices, shards(): memory = lax.all_to_all(scanned, 'seq', 0, 0, tiled=True)  8.74 us
    pallas_call x1, Pallas kernels, attend_swapped(): pl.pallas_call(swapped_kernel, name='swapped', compiler_params=pltpu.Comp...  6.18 us
    pallas_call x1, Pallas kernels, attend_shifted(): pl.pallas_call(shifted_kernel, name='shifted', compiler_params=pltpu.Comp...  5.6 us
  transfers between devices with their start and end apart: 5, of which 4 were waited for; matrix products, arithmetic and copies ran while one was open for 0% of the time, Pallas kernels for 10%

profile of v5, /device:TPU:1, one launch (start us, length us, event | category | flops | bytes accessed | tf_op | source)
XLA Modules:
  0.0 137.8 jit_solution(3826605151329092371)
XLA Ops:
  0.6 1.6 %pieces.1.own_ref = bf16[8,128,256]{2,1,0:T(8,128)(2,1)} custom-call(s32[1]{0:T(128)} %bitcast.2.place_ref, bf16[128,768]{1,0:T(8,128)(2,1)} %key_ref.5, bf16[128,768]{1,0:T(8,128)(2,1)} %value_ref.5), custom_call_target="tpu_custom_call" | custom-call | tf_op jit(solution)/shard_map/pieces/pallas_call | solution.py:300
  2.3 17.5 %all_to_all.20.column_ref.zero_ref = bf16[8,128,256]{2,1,0:T(8,128)(2,1)} all-to-all(bf16[8,128,256]{2,1,0:T(8,128)(2,1)} %pieces.1.own_ref), channel_id=1, replica_groups={{0,96,192,288,384,480,576,672},{396,492,588,684,12,108,204,300},{24,120..., dimensions={0} | all-to-all | bytes 1048576 | tf_op jit(solution)/shard_map/all_to_all | solution.py:384
  19.8 10.1 %collective-permute-start = (bf16[8,128,256]{2,1,0:T(8,128)(2,1)}, bf16[8,128,256]{2,1,0:T(8,128)(2,1)}, u32[]{:S(2)}, u32[]{:S(2)}) collective-permute-start(bf16[8,128,256]{2,1,0:T(8,128)(2,1)} %all_to_all.20.column_ref.zero_ref), channel_id=1, source_target_pairs={{0,24},{12,84},{24,48},{36,12},{48,72},{60,36},{72,0},{84,60},{96,... | collective-permute-start | bytes 1572872 | tf_op jit(solution)/shard_map/ppermute | solution.py:387
  30.0 1.9 %collective-permute-start.2 = (bf16[8,128,256]{2,1,0:T(8,128)(2,1)}, bf16[8,128,256]{2,1,0:T(8,128)(2,1)}, u32[]{:S(2)}, u32[]{:S(2)}) collective-permute-start(bf16[8,128,256]{2,1,0:T(8,128)(2,1)} %all_to_all.20.column_ref.zero_ref), channel_id=1, source_target_pairs={{24,0},{84,12},{48,24},{12,36},{72,48},{36,60},{0,72},{60,84},{120... | collective-permute-start | bytes 1572872 | tf_op jit(solution)/shard_map/ppermute | solution.py:388
  31.9 4.5 %collective-permute-done.one_ref = bf16[8,128,256]{2,1,0:T(8,128)(2,1)} collective-permute-done((bf16[8,128,256]{2,1,0:T(8,128)(2,1)}, bf16[8,128,256]{2,1,0:T(8,128)(2,1)}, u32[]{:S(2)}, u32[]{:S(2)}) %collective-permute-start) | collective-permute-done | bytes 524320 | tf_op jit(solution)/shard_map/ppermute | solution.py:387
  36.4 5.0 %collective-permute-start.1 = (bf16[8,128,256]{2,1,0:T(8,128)(2,1)}, bf16[8,128,256]{2,1,0:T(8,128)(2,1)}, u32[]{:S(2)}, u32[]{:S(2)}) collective-permute-start(bf16[8,128,256]{2,1,0:T(8,128)(2,1)} %collective-permute-done.one_ref), channel_id=1, source_target_pairs={{0,24},{12,84},{24,48},{36,12},{48,72},{60,36},{72,0},{84,60},{96,... | collective-permute-start | bytes 1572872 | tf_op jit(solution)/shard_map/ppermute | solution.py:389
  41.4 3.3 %own.1 = (f32[512,128]{1,0:T(8,128)}, f32[512,128]{1,0:T(8,128)}, f32[512,128]{1,0:T(8,128)}) custom-call(s32[64]{0:T(128)} %seg_ref.5, s32[1]{0:T(128)} %bitcast.1.place_ref, bf16[128,512]{1,0:T(8,128)(2,1)} %query_ref.9, bf16[8,128,256]{2,1,0:T(8,128)(2,1)} %pieces.1.own_ref, bf16[8,128,256]{2,1,0:T(8,128)(2,1)} %all_to_all.20.column_ref.zero_ref), custom_call_target="tpu_custom_call" | custom-call | tf_op jit(solution)/shard_map/own/pallas_call | solution.py:331
  44.7 2.1 %collective-permute-done.2.three_ref = bf16[8,128,256]{2,1,0:T(8,128)(2,1)} collective-permute-done((bf16[8,128,256]{2,1,0:T(8,128)(2,1)}, bf16[8,128,256]{2,1,0:T(8,128)(2,1)}, u32[]{:S(2)}, u32[]{:S(2)}) %collective-permute-start.2) | collective-permute-done | bytes 524320 | tf_op jit(solution)/shard_map/ppermute | solution.py:388
  46.8 2.5 %collective-permute-done.1.two_ref = bf16[8,128,256]{2,1,0:T(8,128)(2,1)} collective-permute-done((bf16[8,128,256]{2,1,0:T(8,128)(2,1)}, bf16[8,128,256]{2,1,0:T(8,128)(2,1)}, u32[]{:S(2)}, u32[]{:S(2)}) %collective-permute-start.1) | collective-permute-done | bytes 524320 | tf_op jit(solution)/shard_map/ppermute | solution.py:389
  49.3 5.6 %shifted.1 = (f32[512,128]{1,0:T(8,128)}, f32[512,128]{1,0:T(8,128)}, f32[512,128]{1,0:T(8,128)}, bf16[32,128,256]{2,1,0:T(8,128)(2,1)}) custom-call(s32[64]{0:T(128)} %seg_ref.5, s32[1]{0:T(128)} %bitcast.1.place_ref, bf16[128,512]{1,0:T(8,128)(2,1)} %query_ref.9, bf16[8,128,256]{2,1,0:T(8,128)(2,1)} %all_to_all.20.column_ref.zero_ref, ...), custom_call_target="tpu_custom_call" | custom-call | tf_op jit(solution)/shard_map/shifted/pallas_call | solution.py:345
  54.9 12.9 %collective-permute-start.3 = (bf16[32,128,256]{2,1,0:T(8,128)(2,1)}, bf16[32,128,256]{2,1,0:T(8,128)(2,1)}, u32[]{:S(2)}, u32[]{:S(2)}) collective-permute-start(bf16[32,128,256]{2,1,0:T(8,128)(2,1)} %get-tuple-element.16), channel_id=1, source_target_pairs={{0,12},{12,0},{24,36},{36,24},{48,60},{60,48},{72,84},{84,72},{96,... | collective-permute-start | bytes 6291464 | tf_op jit(solution)/shard_map/ppermute | solution.py:401
  67.8 2.0 %memory.1 = bf16[64,16,128]{2,1,0:T(8,128)(2,1)} custom-call(bf16[128,512]{1,0:T(8,128)(2,1)} %key_ref.4, bf16[128,512]{1,0:T(8,128)(2,1)} %value_ref.4, f32[4,128]{1,0:T(4,128)} %log_ref.5), custom_call_target="tpu_custom_call" | custom-call | tf_op jit(solution)/shard_map/memory/pallas_call | solution.py:264
  69.9 18.0 %all_to_all.21.in_ref = bf16[64,16,128]{2,1,0:T(8,128)(2,1)} all-to-all(bf16[64,16,128]{2,1,0:T(8,128)(2,1)} %memory.1), channel_id=1, replica_groups=mesh['seq'=64,'head'=12] {'seq'}, dimensions={0} | all-to-all | bytes 524288 | tf_op jit(solution)/shard_map/all_to_all | solution.py:392
  87.8 2.3 %scan.1 = bf16[64,8,128]{2,1,0:T(8,128)(2,1)} custom-call(bf16[64,16,128]{2,1,0:T(8,128)(2,1)} %all_to_all.21.in_ref), custom_call_target="tpu_custom_call" | custom-call | tf_op jit(solution)/shard_map/scan/pallas_call | solution.py:271
  90.1 5.1 %all-to-all-start.1 = ((bf16[64,8,128]{2,1,0:T(8,128)(2,1)}), bf16[64,8,128]{2,1,0:T(8,128)(2,1)}, u32[]{:S(2)}, u32[]{:S(2)}) async-start(bf16[64,8,128]{2,1,0:T(8,128)(2,1)} %scan.1), calls=%async_computation.1 | async-start | bytes 262144 | tf_op jit(solution)/shard_map/all_to_all | solution.py:394
  95.2 2.5 %inside.1.inside_ref = f32[128,512]{1,0:T(8,128)} custom-call(bf16[128,512]{1,0:T(8,128)(2,1)} %query_ref.6, bf16[128,512]{1,0:T(8,128)(2,1)} %key_ref.4, bf16[128,512]{1,0:T(8,128)(2,1)} %value_ref.4, f32[4,128]{1,0:T(4,128)} %log_ref.5), custom_call_target="tpu_custom_call" | custom-call | tf_op jit(solution)/shard_map/inside/pallas_call | solution.py:278
  97.7 8.7 %all-to-all-done.1.memory_ref = bf16[64,8,128]{2,1,0:T(8,128)(2,1)} async-done(((bf16[64,8,128]{2,1,0:T(8,128)(2,1)}), bf16[64,8,128]{2,1,0:T(8,128)(2,1)}, u32[]{:S(2)}, u32[]{:S(2)}) %all-to-all-start.1) | async-done | bytes 131104 | tf_op jit(solution)/shard_map/all_to_all | solution.py:394
  106.4 2.0 %mixed.1 = (f32[128,512]{1,0:T(8,128)}, f32[12,8,128]{2,1,0:T(8,128)}) custom-call(bf16[128,512]{1,0:T(8,128)(2,1)} %query_ref.6, f32[4,128]{1,0:T(4,128)} %log_ref.5, f32[128,512]{1,0:T(8,128)} %inside.1.inside_ref, bf16[64,8,128]{2,1,0:T(8,128)(2,1)} %all-to-all-done.1.memory_ref), custom_call_target="tpu_custom_call" | custom-call | tf_op jit(solution)/shard_map/mixed/pallas_call | solution.py:285
  108.4 21.4 %all_to_all.22.square_ref = f32[12,8,128]{2,1,0:T(8,128)} all-to-all(f32[12,8,128]{2,1,0:T(8,128)} %get-tuple-element.12), channel_id=1, replica_groups=mesh['seq'=64,'head'=12] {'head'}, dimensions={0} | all-to-all | bytes 98304 | tf_op jit(solution)/shard_map/all_to_all | solution.py:397
  129.8 1.8 %gate.1 = bf16[128,512]{1,0:T(8,128)(2,1)} custom-call(f32[128,512]{1,0:T(8,128)} %get-tuple-element.11.mixed_ref, f32[12,8,128]{2,1,0:T(8,128)} %all_to_all.22.square_ref, f32[1,512]{1,0:T(1,128)} %bitcast.3, bf16[128,512]{1,0:T(8,128)(2,1)} %gate_ref.1), custom_call_target="tpu_custom_call" | custom-call | tf_op jit(solution)/shard_map/gate/pallas_call | solution.py:293
  131.7 0.0 collective-permute-done.3.pairs_ref
  131.7 6.2 %swapped.1 = bf16[128,512]{1,0:T(8,128)(2,1)} custom-call(s32[64]{0:T(128)} %seg_ref.5, s32[1]{0:T(128)} %bitcast.1.place_ref, bf16[128,512]{1,0:T(8,128)(2,1)} %query_ref.9, bf16[32,128,256]{2,1,0:T(8,128)(2,1)} %collective-permute-done.3.pairs_ref, f32[512,128]{1,0:T(8,128)} %get-tuple-element.17.old_peak_ref, f32[512,128]{1,0:T(8,128)} %get-tuple-element.18.old_total_ref, ...), custom_call_target="tpu_custom_call" | custom-call | tf_op jit(solution)/shard_map/swapped/pallas_call | solution.py:354
Async XLA Ops:
  19.8 16.6 %collective-permute-start = (bf16[8,128,256]{2,1,0:T(8,128)(2,1)}, bf16[8,128,256]{2,1,0:T(8,128)(2,1)}, u32[]{:S(2)}, u32[]{:S(2)}) collective-permute-start(bf16[8,128,256]{2,1,0:T(8,128)(2,1)} %all_to_all.20.column_ref.zero_ref), channel_id=1, source_target_pairs={{0,24},{12,84},{24,48},{36,12},{48,72},{60,36},{72,0},{84,60},{96,... | collective-permute-start | bytes 1572872 | tf_op jit(solution)/shard_map/ppermute | solution.py:387
  30.0 16.8 %collective-permute-start.2 = (bf16[8,128,256]{2,1,0:T(8,128)(2,1)}, bf16[8,128,256]{2,1,0:T(8,128)(2,1)}, u32[]{:S(2)}, u32[]{:S(2)}) collective-permute-start(bf16[8,128,256]{2,1,0:T(8,128)(2,1)} %all_to_all.20.column_ref.zero_ref), channel_id=1, source_target_pairs={{24,0},{84,12},{48,24},{12,36},{72,48},{36,60},{0,72},{60,84},{120... | collective-permute-start | bytes 1572872 | tf_op jit(solution)/shard_map/ppermute | solution.py:388
  36.4 12.9 %collective-permute-start.1 = (bf16[8,128,256]{2,1,0:T(8,128)(2,1)}, bf16[8,128,256]{2,1,0:T(8,128)(2,1)}, u32[]{:S(2)}, u32[]{:S(2)}) collective-permute-start(bf16[8,128,256]{2,1,0:T(8,128)(2,1)} %collective-permute-done.one_ref), channel_id=1, source_target_pairs={{0,24},{12,84},{24,48},{36,12},{48,72},{60,36},{72,0},{84,60},{96,... | collective-permute-start | bytes 1572872 | tf_op jit(solution)/shard_map/ppermute | solution.py:389
  54.9 76.7 %collective-permute-start.3 = (bf16[32,128,256]{2,1,0:T(8,128)(2,1)}, bf16[32,128,256]{2,1,0:T(8,128)(2,1)}, u32[]{:S(2)}, u32[]{:S(2)}) collective-permute-start(bf16[32,128,256]{2,1,0:T(8,128)(2,1)} %get-tuple-element.16), channel_id=1, source_target_pairs={{0,12},{12,0},{24,36},{36,24},{48,60},{60,48},{72,84},{84,72},{96,... | collective-permute-start | bytes 6291464 | tf_op jit(solution)/shard_map/ppermute | solution.py:401
  90.1 16.4 %all-to-all-start.1 = ((bf16[64,8,128]{2,1,0:T(8,128)(2,1)}), bf16[64,8,128]{2,1,0:T(8,128)(2,1)}, u32[]{:S(2)}, u32[]{:S(2)}) async-start(bf16[64,8,128]{2,1,0:T(8,128)(2,1)} %scan.1), calls=%async_computation.1 | async-start | bytes 262144 | tf_op jit(solution)/shard_map/all_to_all | solution.py:394
